TPU v7x, 256 devices: a whole 4x4x8 slice. The times are simulated.
256 devices in a mesh: row: 8 (over z_lo, core), col: 32 (over z_hi, x, y).
Axes of the slice: x: 4, y: 4, z: 8 (z_hi: 2, z_lo: 4; z = z_hi * 4 + z_lo), core: 2. Of those that a mesh axis runs over, the one named last changes fastest.
Arguments:
- covariance: float32 [8192, 8192], P('row', 'col'), may hold values from -12 to 12, as said below
- noise_var: float32 [64, 128], P('row'), may hold values from 0.1 to 1
- wind_table: float32 [16, 2], replicated, may hold values from -0.7 to 0.7
- diffusivity: float32 [16], replicated, may hold values from 0.01 to 0.05
- wind_index: int32 [3, 64], replicated, may hold values from 0 to 15
Outputs:
- predicted_spread_matrix: float32 [8192, 8192], P('row', 'col')
- operator_times_prior: bfloat16 [8192, 8192], P('row', 'col')
Inputs may be any that keep to these rules, and one draw needn't show every extreme that they name: covariance is symmetric: entry (a, b) equals entry (b, a) exactly.
All inputs are finite; a program needn't handle non-finite values.
Results may differ from a plain program's by a relative error of at most 0.0025.
Values may be sent and summed in bfloat16 or wider, within the bound.
A program may use at most 64 MiB of HBM per device.

v0:
```python
import jax
import jax.numpy as jnp
from jax import lax
from jax.sharding import PartitionSpec as P


def with_halo(shard, sides, width):
    for axis, dim in sides:
        size, length = (lax.axis_size(axis), shard.shape[dim])
        up = [(i, (i + 1) % size) for i in range(size - 1)]
        down = [(j, i) for i, j in up]
        last = lax.slice_in_dim(shard, length - width, length, axis=dim)
        initial = lax.slice_in_dim(shard, 0, width, axis=dim)
        before = lax.ppermute(last, axis, up)
        after = lax.ppermute(initial, axis, down)
        shard = jnp.concatenate([before, shard, after], axis=dim)
    return shard


def stencil_terms(zonal_cour, merid_cour, diffuse):
    middle_weight = 1.0 - zonal_cour * zonal_cour - merid_cour * merid_cour - 4.0 * diffuse
    eastward_weight = 0.5 * zonal_cour * zonal_cour - 0.5 * zonal_cour + diffuse
    west_w = 0.5 * zonal_cour * zonal_cour + 0.5 * zonal_cour + diffuse
    north_w = 0.5 * merid_cour * merid_cour - 0.5 * merid_cour + diffuse
    south_w = 0.5 * merid_cour * merid_cour + 0.5 * merid_cour + diffuse
    return jnp.stack([middle_weight, eastward_weight, west_w, north_w, south_w])


def looked_up(wind_table, diffusivity, wind_index):
    table_ids = jnp.arange(wind_table.shape[0], dtype=jnp.int32)
    one_hot = (wind_index[:, :, None] == table_ids[None, None, :]).astype(jnp.float32)
    courant = jnp.einsum("sly,yc->slc", one_hot, wind_table, precision=lax.Precision.HIGHEST)
    diffuse = jnp.einsum("sly,y->sl", one_hot, diffusivity, precision=lax.Precision.HIGHEST)
    return stencil_terms(courant[..., 0], courant[..., 1], diffuse)


def strip_steps(values, padded_w, first_lat):
    steps = padded_w.shape[1]
    for step_no in range(steps):
        span = values.shape[0] - 2
        terms = lax.dynamic_slice_in_dim(padded_w[:, step_no], first_lat + 1 + steps, span, 1)
        middle_weight, eastward_weight, west_w, north_w, south_w = [
            terms[member][:, None, None] for member in range(5)
        ]
        middle = values[1:-1]
        values = (
            middle_weight * middle
            + eastward_weight * jnp.roll(middle, -1, 1)
            + west_w * jnp.roll(middle, 1, 1)
            + north_w * values[2:]
            + south_w * values[:-2]
        )
        first_lat = first_lat + 1
    return values


def from_symmetry(covariance, padded_w, nlon):
    rows_dev, cols_dev = covariance.shape
    steps = padded_w.shape[1]
    parallel_columns = cols_dev // nlon
    first_col = lax.axis_index("col") * parallel_columns
    values = covariance.reshape(rows_dev, parallel_columns, nlon)
    for step_no in range(steps):
        widened = with_halo(values, (("col", 1),), 1)
        terms = lax.dynamic_slice_in_dim(
            padded_w[:, step_no], first_col + steps, parallel_columns, 1
        )
        middle_weight, eastward_weight, west_w, north_w, south_w = [
            terms[member][None, :, None] for member in range(5)
        ]
        values = (
            middle_weight * values
            + eastward_weight * jnp.roll(values, -1, 2)
            + west_w * jnp.roll(values, 1, 2)
            + north_w * widened[:, 2:]
            + south_w * widened[:, :-2]
        )
    return values.reshape(rows_dev, cols_dev).astype(jnp.bfloat16)


def body(covariance, noise_var, wind_table, diffusivity, wind_index):
    rows_dev, cols_dev = covariance.shape
    lat_rows, nlon = noise_var.shape
    steps = wind_index.shape[0]
    weights = looked_up(wind_table, diffusivity, wind_index)
    padded_w = jnp.pad(weights, ((0, 0), (0, 0), (steps, steps)))
    row_id = lax.axis_index("row")
    col_id = lax.axis_index("col")
    first_lat = row_id * lat_rows - steps
    widened = with_halo(covariance.reshape(lat_rows, nlon, cols_dev), (("row", 0),), steps)
    operator_times_prior = (
        strip_steps(widened, padded_w, first_lat).reshape(rows_dev, cols_dev).astype(jnp.bfloat16)
    )
    s_mirror = from_symmetry(covariance, padded_w, nlon)
    widened_s = with_halo(s_mirror.reshape(lat_rows, nlon, cols_dev), (("row", 0),), steps)
    output_matrix = strip_steps(widened_s.astype(jnp.float32), padded_w, first_lat).reshape(
        rows_dev, cols_dev
    )
    global_rows = row_id * rows_dev + jnp.arange(rows_dev, dtype=jnp.int32)
    global_cols = col_id * cols_dev + jnp.arange(cols_dev, dtype=jnp.int32)
    on_diag = global_rows[:, None] == global_cols[None, :]
    noise_flat = noise_var.reshape(rows_dev)
    predicted_spread_matrix = output_matrix + jnp.where(
        on_diag, noise_flat[:, None], jnp.zeros((), jnp.float32)
    )
    return (predicted_spread_matrix, operator_times_prior)


def solution(mesh):
    in_specs = (P("row", "col"), P("row", None), P(), P(), P())
    out_specs = (P("row", "col"), P("row", "col"))
    return jax.shard_map(body, mesh=mesh, in_specs=in_specs, out_specs=out_specs, check_vma=False)
```

profile of v0, /device:TPU:129, one launch (start us, length us, event | category | flops | bytes accessed | tf_op | source)
XLA Modules:
  0.0 141.1 jit_solution(16741774553940593923)
XLA Ops:
  0.6 1.7 %reshape.134 = f32[1024,2,128]{2,1,0:T(2,128)S(1)} reshape(f32[1024,256]{1,0:T(8,128)} %param.5) | data formatting | bytes 2097152 | tf_op jit(solution)/shard_map/reshape | solution.py:62
  2.4 1.8 %fusion.116 = (f32[1024,1,128]{2,1,0:T(1,128)}, f32[1024,1,128]{2,1,0:T(1,128)}) fusion(f32[1024,2,128]{2,1,0:T(2,128)S(1)} %reshape.134), kind=kLoop, calls=%fused_computation.213 | loop fusion | bytes 2097152 | tf_op jit(solution)/shard_map/slice | solution.py:13
  4.2 5.0 %collective-permute-start = (f32[1024,1,128]{2,1,0:T(1,128)}, f32[1024,1,128]{2,1,0:T(1,128)}, u32[]{:S(2)}, u32[]{:S(2)}) collective-permute-start(f32[1024,1,128]{2,1,0:T(1,128)} %get-tuple-element.40), channel_id=1, source_target_pairs={{1,0},{2,1},{3,2},{4,3},{5,4},{6,5},{7,6},{8,7},{9,8},{10,9},{11,1... | collective-permute-start | bytes 1572872 | tf_op jit(solution)/shard_map/ppermute | solution.py:15
  9.2 1.9 %collective-permute-start.1 = (f32[1024,1,128]{2,1,0:T(1,128)}, f32[1024,1,128]{2,1,0:T(1,128)}, u32[]{:S(2)}, u32[]{:S(2)}) collective-permute-start(f32[1024,1,128]{2,1,0:T(1,128)} %get-tuple-element.41), channel_id=1, source_target_pairs={{0,1},{1,2},{2,3},{3,4},{4,5},{5,6},{6,7},{7,8},{8,9},{9,10},{10,1... | collective-permute-start | bytes 1572872 | tf_op jit(solution)/shard_map/ppermute | solution.py:14
  12.0 4.4 %collective-permute-start.8 = (f32[3,128,256]{2,1,0:T(8,128)}, f32[3,128,256]{2,1,0:T(8,128)S(1)}, u32[]{:S(2)}, u32[]{:S(2)}) collective-permute-start(f32[3,128,256]{2,1,0:T(8,128)} %bitcast.41), channel_id=1, source_target_pairs={{0,32},{32,64},{64,96},{96,128},{128,160},{160,192},{192,224},{1,3... | collective-permute-start | bytes 1179656 | tf_op jit(solution)/shard_map/ppermute | solution.py:14
  16.3 1.9 %collective-permute-start.9 = (f32[3,128,256]{2,1,0:T(8,128)S(1)}, f32[3,128,256]{2,1,0:T(8,128)S(1)}, u32[]{:S(2)}, u32[]{:S(2)}) collective-permute-start(f32[3,128,256]{2,1,0:T(8,128)S(1)} %bitcast.128), channel_id=1, source_target_pairs={{32,0},{64,32},{96,64},{128,96},{160,128},{192,160},{224,192},{33,... | collective-permute-start | bytes 1179656 | tf_op jit(solution)/shard_map/ppermute | solution.py:15
  18.3 2.4 %fusion.114 = (f32[1024,2,1]{2,1,0:T(2,128)}, f32[1024,2,1]{2,1,0:T(2,128)}) fusion(f32[1024,2,128]{2,1,0:T(2,128)S(1)} %reshape.134), kind=kLoop, calls=%fused_computation.211 | loop fusion | bytes 32768 | tf_op jit(solution)/shard_map/jit(_roll_static)/slice | solution.py:74
  23.4 1.1 fusion.115
  25.5 13.1 %collective-permute-done.9 = f32[3,128,256]{2,1,0:T(8,128)S(1)} collective-permute-done((f32[3,128,256]{2,1,0:T(8,128)S(1)}, f32[3,128,256]{2,1,0:T(8,128)S(1)}, u32[]{:S(2)}, u32[]{:S(2)}) %collective-permute-start.9) | collective-permute-done | bytes 393248 | tf_op jit(solution)/shard_map/ppermute | solution.py:15
  40.1 1.7 %fusion = f32[12,128,256]{2,1,0:T(8,128)S(1)} fusion(f32[14,128,256]{2,1,0:T(8,128)S(1)} %pad_maximum_fusion, f32[3,128,256]{2,1,0:T(8,128)S(1)} %collective-permute-done.9, f32[8,128,256]{2,1,0:T(8,128)S(1)} %bitcast.126, f32[3,128,256]{2,1,0:T(8,128)S(1)} %collective-permute-done.8, f32[12,127,256]{2,1,0:T(8,128)S(1)} %get-tuple-element.3, ...), kind=kLoop, calls=%fused_computation.2 | loop fusion | flops 5898240 | bytes 11247856 | tf_op jit(solution)/shard_map/add | solution.py:47
  41.8 1.7 %fusion.100 = (f32[10,127,256]{2,1,0:T(8,128)}, f32[10,127,256]{2,1,0:T(8,128)}) fusion(f32[12,128,256]{2,1,0:T(8,128)S(1)} %fusion), kind=kLoop, calls=%fused_computation.197 | loop fusion | bytes 5201920 | tf_op jit(solution)/shard_map/jit(_roll_static)/slice | solution.py:49
  44.3 5.6 %fusion.38 = f32[1024,2,128]{2,1,0:T(2,128)S(1)} fusion(f32[1024,2,128]{2,1,0:T(2,128)S(1)} %reshape.134, f32[1024,1,128]{2,1,0:T(1,128)} %collective-permute-done.1, f32[1024,1,128]{2,1,0:T(1,128)} %collective-permute-done, f32[1024,2,1]{2,1,0:T(2,128)S(1)} %copy-done.6, f32[1024,2,127]{2,1,0:T(2,128)S(1)} %get-tuple-element.39, ...), kind=kLoop, calls=%fused_computation.72 | loop fusion | flops 3407872 | bytes 5242920 | tf_op jit(solution)/shard_map/add | solution.py:72
  50.7 13.4 %collective-permute-start.2 = (f32[1024,1,128]{2,1,0:T(1,128)S(1)}, f32[1024,1,128]{2,1,0:T(1,128)S(1)}, u32[]{:S(2)}, u32[]{:S(2)}) collective-permute-start(f32[1024,1,128]{2,1,0:T(1,128)S(1)} %get-tuple-element.34), channel_id=1, source_target_pairs={{1,0},{2,1},{3,2},{4,3},{5,4},{6,5},{7,6},{8,7},{9,8},{10,9},{11,1... | collective-permute-start | bytes 1572872 | tf_op jit(solution)/shard_map/ppermute | solution.py:15
  64.1 2.1 %collective-permute-start.3 = (f32[1024,1,128]{2,1,0:T(1,128)S(1)}, f32[1024,1,128]{2,1,0:T(1,128)S(1)}, u32[]{:S(2)}, u32[]{:S(2)}) collective-permute-start(f32[1024,1,128]{2,1,0:T(1,128)S(1)} %get-tuple-element.35), channel_id=1, source_target_pairs={{0,1},{1,2},{2,3},{3,4},{4,5},{5,6},{6,7},{7,8},{8,9},{9,10},{10,1... | collective-permute-start | bytes 1572872 | tf_op jit(solution)/shard_map/ppermute | solution.py:14
  66.2 1.1 fusion.111
  67.4 1.1 fusion.112
  68.5 1.7 %collective-permute-done.2 = f32[1024,1,128]{2,1,0:T(1,128)S(1)} collective-permute-done((f32[1024,1,128]{2,1,0:T(1,128)S(1)}, f32[1024,1,128]{2,1,0:T(1,128)S(1)}, u32[]{:S(2)}, u32[]{:S(2)}) %collective-permute-start.2) | collective-permute-done | bytes 524320 | tf_op jit(solution)/shard_map/ppermute | solution.py:15
  70.2 12.0 %collective-permute-done.3 = f32[1024,1,128]{2,1,0:T(1,128)S(1)} collective-permute-done((f32[1024,1,128]{2,1,0:T(1,128)S(1)}, f32[1024,1,128]{2,1,0:T(1,128)S(1)}, u32[]{:S(2)}, u32[]{:S(2)}) %collective-permute-start.3) | collective-permute-done | bytes 524320 | tf_op jit(solution)/shard_map/ppermute | solution.py:14
  82.3 4.6 %fusion.34 = f32[1024,2,128]{2,1,0:T(2,128)S(1)} fusion(f32[1024,2,128]{2,1,0:T(2,128)S(1)} %fusion.38, f32[1024,1,128]{2,1,0:T(1,128)S(1)} %collective-permute-done.3, f32[1024,1,128]{2,1,0:T(1,128)S(1)} %collective-permute-done.2, f32[1024,2,1]{2,1,0:T(2,128)S(1)} %get-tuple-element.31, f32[1024,2,127]{2,1,0:T(2,128)S(1)} %get-tuple-element.33, ...), kind=kLoop, calls=%fused_computation.66 | loop fusion | flops 3407872 | bytes 5242920 | tf_op jit(solution)/shard_map/add | solution.py:72
  87.7 1.9 %collective-permute-start.4 = (f32[1024,1,128]{2,1,0:T(1,128)S(1)}, f32[1024,1,128]{2,1,0:T(1,128)S(1)}, u32[]{:S(2)}, u32[]{:S(2)}) collective-permute-start(f32[1024,1,128]{2,1,0:T(1,128)S(1)} %get-tuple-element.28), channel_id=1, source_target_pairs={{1,0},{2,1},{3,2},{4,3},{5,4},{6,5},{7,6},{8,7},{9,8},{10,9},{11,1... | collective-permute-start | bytes 1572872 | tf_op jit(solution)/shard_map/ppermute | solution.py:15
  89.6 3.4 %collective-permute-start.5 = (f32[1024,1,128]{2,1,0:T(1,128)S(1)}, f32[1024,1,128]{2,1,0:T(1,128)S(1)}, u32[]{:S(2)}, u32[]{:S(2)}) collective-permute-start(f32[1024,1,128]{2,1,0:T(1,128)S(1)} %get-tuple-element.29), channel_id=1, source_target_pairs={{0,1},{1,2},{2,3},{3,4},{4,5},{5,6},{6,7},{7,8},{8,9},{9,10},{10,1... | collective-permute-start | bytes 1572872 | tf_op jit(solution)/shard_map/ppermute | solution.py:14
  93.0 1.1 fusion.108
  94.1 1.1 fusion.109
  95.3 2.3 %collective-permute-done.4 = f32[1024,1,128]{2,1,0:T(1,128)S(1)} collective-permute-done((f32[1024,1,128]{2,1,0:T(1,128)S(1)}, f32[1024,1,128]{2,1,0:T(1,128)S(1)}, u32[]{:S(2)}, u32[]{:S(2)}) %collective-permute-start.4) | collective-permute-done | bytes 524320 | tf_op jit(solution)/shard_map/ppermute | solution.py:15
  97.6 10.1 %collective-permute-done.5 = f32[1024,1,128]{2,1,0:T(1,128)S(1)} collective-permute-done((f32[1024,1,128]{2,1,0:T(1,128)S(1)}, f32[1024,1,128]{2,1,0:T(1,128)S(1)}, u32[]{:S(2)}, u32[]{:S(2)}) %collective-permute-start.5) | collective-permute-done | bytes 524320 | tf_op jit(solution)/shard_map/ppermute | solution.py:14
  107.7 4.7 %fusion.47 = bf16[1024,2,128]{2,1,0:T(2,128)(2,1)S(1)} fusion(f32[1024,2,128]{2,1,0:T(2,128)S(1)} %fusion.34, f32[1024,1,128]{2,1,0:T(1,128)S(1)} %collective-permute-done.5, f32[1024,1,128]{2,1,0:T(1,128)S(1)} %collective-permute-done.4, f32[1024,2,127]{2,1,0:T(2,128)S(1)} %get-tuple-element.25, f32[1024,2,1]{2,1,0:T(2,128)S(1)} %get-tuple-element.27, ...), kind=kLoop, calls=%fused_computation.93 | loop fusion | flops 3670016 | bytes 4718632 | tf_op jit(solution)/shard_map/convert_element_type | solution.py:78
  112.8 12.3 %collective-permute-start.6 = (bf16[3,128,256]{2,1,0:T(8,128)(2,1)S(1)}, bf16[3,128,256]{2,1,0:T(8,128)(2,1)S(1)}, u32[]{:S(2)}, u32[]{:S(2)}) collective-permute-start(bf16[3,128,256]{2,1,0:T(8,128)(2,1)S(1)} %slice.474), channel_id=1, source_target_pairs={{0,32},{32,64},{64,96},{96,128},{128,160},{160,192},{192,224},{1,3... | collective-permute-start | bytes 589832 | tf_op jit(solution)/shard_map/ppermute | solution.py:14
  125.2 2.1 %collective-permute-start.7 = (bf16[3,128,256]{2,1,0:T(8,128)(2,1)S(1)}, bf16[3,128,256]{2,1,0:T(8,128)(2,1)S(1)}, u32[]{:S(2)}, u32[]{:S(2)}) collective-permute-start(bf16[3,128,256]{2,1,0:T(8,128)(2,1)S(1)} %slice.476), channel_id=1, source_target_pairs={{32,0},{64,32},{96,64},{128,96},{160,128},{192,160},{224,192},{33,... | collective-permute-start | bytes 589832 | tf_op jit(solution)/shard_map/ppermute | solution.py:15
  127.8 4.5 %collective-permute-done.7 = bf16[3,128,256]{2,1,0:T(8,128)(2,1)S(1)} collective-permute-done((bf16[3,128,256]{2,1,0:T(8,128)(2,1)S(1)}, bf16[3,128,256]{2,1,0:T(8,128)(2,1)S(1)}, u32[]{:S(2)}, u32[]{:S(2)}) %collective-permute-start.7) | collective-permute-done | bytes 196640 | tf_op jit(solution)/shard_map/ppermute | solution.py:15
  135.7 1.5 %fusion.12 = (f32[10,128,256]{2,1,0:T(8,128)S(1)}, f32[10,128,256]{2,1,0:T(8,128)S(1)}) fusion(f32[12,128,256]{2,1,0:T(8,128)S(1)} %fusion, f32[10,1,256]{2,1,0:T(1,128)S(1)} %get-tuple-element.7, f32[10,127,256]{2,1,0:T(8,128)S(1)} %copy-done.4, f32[10,127,256]{2,1,0:T(8,128)S(1)} %copy-done.3, f32[10,1,256]{2,1,0:T(1,128)S(1)} %get-tuple-element.6, ...), kind=kLoop, calls=%fused_computation.26 | loop fusion | flops 7208960 | bytes 15728840 | tf_op jit(solution)/shard_map/add | solution.py:47
  137.9 1.8 %fusion.21 = (bf16[8,128,256]{2,1,0:T(8,128)(2,1)}, f32[8,128,256]{2,1,0:T(8,128)S(1)}) fusion(f32[10,128,256]{2,1,0:T(8,128)S(1)} %get-tuple-element.53, f32[8,1,256]{2,1,0:T(1,128)S(1)} %get-tuple-element.15, f32[8,127,256]{2,1,0:T(8,128)S(1)} %get-tuple-element.17, f32[8,127,256]{2,1,0:T(8,128)S(1)} %get-tuple-element.16, ...), kind=kLoop, calls=%fused_computation.45 | loop fusion | flops 6029312 | bytes 12058784 | tf_op jit(solution)/shard_map/convert_element_type | solution.py:92
  139.8 1.3 bitcast_add_fusion
  (93 shorter events, 13.1 us)
Async XLA Ops:
  0.6 20.2 %copy-start = (f32[16,2]{0,1:T(2,128)S(1)}, f32[16,2]{0,1:T(2,128)}, u32[]{:S(2)}) copy-start(f32[16,2]{0,1:T(2,128)} %param.7) | copy-start | bytes 388
  2.4 8.7 %copy-start.1 = (f32[1024,256]{1,0:T(8,128)S(1)}, f32[1024,256]{1,0:T(8,128)}, u32[]{:S(2)}) copy-start(f32[1024,256]{1,0:T(8,128)} %param.5) | copy-start | bytes 3145732
  4.2 39.3 %collective-permute-start = (f32[1024,1,128]{2,1,0:T(1,128)}, f32[1024,1,128]{2,1,0:T(1,128)}, u32[]{:S(2)}, u32[]{:S(2)}) collective-permute-start(f32[1024,1,128]{2,1,0:T(1,128)} %get-tuple-element.40), channel_id=1, source_target_pairs={{1,0},{2,1},{3,2},{4,3},{5,4},{6,5},{7,6},{8,7},{9,8},{10,9},{11,1... | collective-permute-start | bytes 1572872 | tf_op jit(solution)/shard_map/ppermute | solution.py:15
  9.2 34.3 %collective-permute-start.1 = (f32[1024,1,128]{2,1,0:T(1,128)}, f32[1024,1,128]{2,1,0:T(1,128)}, u32[]{:S(2)}, u32[]{:S(2)}) collective-permute-start(f32[1024,1,128]{2,1,0:T(1,128)} %get-tuple-element.41), channel_id=1, source_target_pairs={{0,1},{1,2},{2,3},{3,4},{4,5},{5,6},{6,7},{7,8},{8,9},{9,10},{10,1... | collective-permute-start | bytes 1572872 | tf_op jit(solution)/shard_map/ppermute | solution.py:14
  12.0 13.6 %collective-permute-start.8 = (f32[3,128,256]{2,1,0:T(8,128)}, f32[3,128,256]{2,1,0:T(8,128)S(1)}, u32[]{:S(2)}, u32[]{:S(2)}) collective-permute-start(f32[3,128,256]{2,1,0:T(8,128)} %bitcast.41), channel_id=1, source_target_pairs={{0,32},{32,64},{64,96},{96,128},{128,160},{160,192},{192,224},{1,3... | collective-permute-start | bytes 1179656 | tf_op jit(solution)/shard_map/ppermute | solution.py:14
  16.3 22.3 %collective-permute-start.9 = (f32[3,128,256]{2,1,0:T(8,128)S(1)}, f32[3,128,256]{2,1,0:T(8,128)S(1)}, u32[]{:S(2)}, u32[]{:S(2)}) collective-permute-start(f32[3,128,256]{2,1,0:T(8,128)S(1)} %bitcast.128), channel_id=1, source_target_pairs={{32,0},{64,32},{96,64},{128,96},{160,128},{192,160},{224,192},{33,... | collective-permute-start | bytes 1179656 | tf_op jit(solution)/shard_map/ppermute | solution.py:15
  18.3 2.5 %copy-start.24 = (s32[3,64]{1,0:T(4,128)S(1)}, s32[3,64]{1,0:T(4,128)}, u32[]{:S(2)}) copy-start(s32[3,64]{1,0:T(4,128)} %param.9) | copy-start | bytes 2308
  18.3 2.5 %copy-start.26 = (f32[16]{0:T(128)S(1)}, f32[16]{0:T(128)}, u32[]{:S(2)}) copy-start(f32[16]{0:T(128)} %param.8) | copy-start | bytes 196
  21.5 17.7 %copy-start.7 = (f32[12]{0:T(128)}, f32[12]{0:T(128)S(1)}, u32[]{:S(2)}) copy-start(f32[12]{0:T(128)S(1)} %get-tuple-element.67) | copy-start | bytes 148
  21.5 17.7 %copy-start.9 = (f32[12]{0:T(128)}, f32[12]{0:T(128)S(1)}, u32[]{:S(2)}) copy-start(f32[12]{0:T(128)S(1)} %get-tuple-element.68) | copy-start | bytes 148
  21.5 17.7 %copy-start.11 = (f32[12]{0:T(128)}, f32[12]{0:T(128)S(1)}, u32[]{:S(2)}) copy-start(f32[12]{0:T(128)S(1)} %get-tuple-element.69) | copy-start | bytes 148
  38.9 1.2 copy-start.2
  41.8 1.7 %copy-start.5 = (f32[1024,2,1]{2,1,0:T(2,128)S(1)}, f32[1024,2,1]{2,1,0:T(2,128)}, u32[]{:S(2)}) copy-start(f32[1024,2,1]{2,1,0:T(2,128)} %get-tuple-element.36) | copy-start | bytes 24580
  41.8 2.5 %copy-start.6 = (f32[1024,2,1]{2,1,0:T(2,128)S(1)}, f32[1024,2,1]{2,1,0:T(2,128)}, u32[]{:S(2)}) copy-start(f32[1024,2,1]{2,1,0:T(2,128)} %get-tuple-element.37) | copy-start | bytes 24580
  50.7 19.5 %collective-permute-start.2 = (f32[1024,1,128]{2,1,0:T(1,128)S(1)}, f32[1024,1,128]{2,1,0:T(1,128)S(1)}, u32[]{:S(2)}, u32[]{:S(2)}) collective-permute-start(f32[1024,1,128]{2,1,0:T(1,128)S(1)} %get-tuple-element.34), channel_id=1, source_target_pairs={{1,0},{2,1},{3,2},{4,3},{5,4},{6,5},{7,6},{8,7},{9,8},{10,9},{11,1... | collective-permute-start | bytes 1572872 | tf_op jit(solution)/shard_map/ppermute | solution.py:15
  64.1 18.2 %collective-permute-start.3 = (f32[1024,1,128]{2,1,0:T(1,128)S(1)}, f32[1024,1,128]{2,1,0:T(1,128)S(1)}, u32[]{:S(2)}, u32[]{:S(2)}) collective-permute-start(f32[1024,1,128]{2,1,0:T(1,128)S(1)} %get-tuple-element.35), channel_id=1, source_target_pairs={{0,1},{1,2},{2,3},{3,4},{4,5},{5,6},{6,7},{7,8},{8,9},{9,10},{10,1... | collective-permute-start | bytes 1572872 | tf_op jit(solution)/shard_map/ppermute | solution.py:14
  87.7 9.9 %collective-permute-start.4 = (f32[1024,1,128]{2,1,0:T(1,128)S(1)}, f32[1024,1,128]{2,1,0:T(1,128)S(1)}, u32[]{:S(2)}, u32[]{:S(2)}) collective-permute-start(f32[1024,1,128]{2,1,0:T(1,128)S(1)} %get-tuple-element.28), channel_id=1, source_target_pairs={{1,0},{2,1},{3,2},{4,3},{5,4},{6,5},{7,6},{8,7},{9,8},{10,9},{11,1... | collective-permute-start | bytes 1572872 | tf_op jit(solution)/shard_map/ppermute | solution.py:15
  89.6 18.1 %collective-permute-start.5 = (f32[1024,1,128]{2,1,0:T(1,128)S(1)}, f32[1024,1,128]{2,1,0:T(1,128)S(1)}, u32[]{:S(2)}, u32[]{:S(2)}) collective-permute-start(f32[1024,1,128]{2,1,0:T(1,128)S(1)} %get-tuple-element.29), channel_id=1, source_target_pairs={{0,1},{1,2},{2,3},{3,4},{4,5},{5,6},{6,7},{7,8},{8,9},{9,10},{10,1... | collective-permute-start | bytes 1572872 | tf_op jit(solution)/shard_map/ppermute | solution.py:14
  112.8 15.0 %collective-permute-start.6 = (bf16[3,128,256]{2,1,0:T(8,128)(2,1)S(1)}, bf16[3,128,256]{2,1,0:T(8,128)(2,1)S(1)}, u32[]{:S(2)}, u32[]{:S(2)}) collective-permute-start(bf16[3,128,256]{2,1,0:T(8,128)(2,1)S(1)} %slice.474), channel_id=1, source_target_pairs={{0,32},{32,64},{64,96},{96,128},{128,160},{160,192},{192,224},{1,3... | collective-permute-start | bytes 589832 | tf_op jit(solution)/shard_map/ppermute | solution.py:14
  125.2 7.0 %collective-permute-start.7 = (bf16[3,128,256]{2,1,0:T(8,128)(2,1)S(1)}, bf16[3,128,256]{2,1,0:T(8,128)(2,1)S(1)}, u32[]{:S(2)}, u32[]{:S(2)}) collective-permute-start(bf16[3,128,256]{2,1,0:T(8,128)(2,1)S(1)} %slice.476), channel_id=1, source_target_pairs={{32,0},{64,32},{96,64},{128,96},{160,128},{192,160},{224,192},{33,... | collective-permute-start | bytes 589832 | tf_op jit(solution)/shard_map/ppermute | solution.py:15
  132.4 0.7 copy-start.12
  133.9 1.3 copy-start.3
  133.9 1.7 %copy-start.4 = (f32[10,127,256]{2,1,0:T(8,128)S(1)}, f32[10,127,256]{2,1,0:T(8,128)}, u32[]{:S(2)}) copy-start(f32[10,127,256]{2,1,0:T(8,128)} %get-tuple-element.9) | copy-start | bytes 3901444
  134.0 1.7 %copy-start.14 = (f32[10]{0:T(128)S(1)}, f32[10]{0:T(128)}, u32[]{:S(2)}) copy-start(f32[10]{0:T(128)} %get-tuple-element.60) | copy-start | bytes 124
  134.0 1.7 %copy-start.15 = (f32[10]{0:T(128)S(1)}, f32[10]{0:T(128)}, u32[]{:S(2)}) copy-start(f32[10]{0:T(128)} %get-tuple-element.61) | copy-start | bytes 124
  134.0 1.7 %copy-start.16 = (f32[10]{0:T(128)S(1)}, f32[10]{0:T(128)}, u32[]{:S(2)}) copy-start(f32[10]{0:T(128)} %get-tuple-element.62) | copy-start | bytes 124
  134.0 1.7 %copy-start.17 = (f32[10]{0:T(128)S(1)}, f32[10]{0:T(128)}, u32[]{:S(2)}) copy-start(f32[10]{0:T(128)} %get-tuple-element.63) | copy-start | bytes 124
  134.0 1.7 %copy-start.18 = (f32[10]{0:T(128)S(1)}, f32[10]{0:T(128)}, u32[]{:S(2)}) copy-start(f32[10]{0:T(128)} %get-tuple-element.64) | copy-start | bytes 124
  137.2 0.7 copy-start.22
  137.3 0.7 copy-start.23
  137.9 1.8 %copy-start.13 = (f32[8,128]{1,0:T(8,128)S(1)}, f32[8,128]{1,0:T(8,128)}, u32[]{:S(2)}) copy-start(f32[8,128]{1,0:T(8,128)} %param.6) | copy-start | bytes 12292
  137.9 1.8 %copy-start.25 = (s32[256]{0:T(256)S(1)}, s32[256]{0:T(256)}, u32[]{:S(2)}) copy-start(s32[256]{0:T(256)} %iota_add_fusion.1) | copy-start | bytes 3076
  (5 other events, 3.1 us)
where the time goes:
time: 142 us; the launch traced here: 141 us
  starting transfers between devices  48.5 us (34%)
  waiting for transfers between devices  44.7 us (31%)
  local copies, waits for them, and re-layouts  23.4 us (16%)
  other arithmetic  23.1 us (16%)
    ppermute x5, starting transfers between devices, with_halo(): after = lax.ppermute(initial, axis, down)  24.4 us
    ppermute x5, starting transfers between devices, with_halo(): before = lax.ppermute(last, axis, up)  24.1 us
    ppermute x5, waiting for transfers between devices, with_halo(): before = lax.ppermute(last, axis, up)  23.1 us
    ppermute x5, waiting for transfers between devices, with_halo(): after = lax.ppermute(initial, axis, down)  21.6 us
    add x2, other arithmetic, from_symmetry(): middle_weight * values + eastward_weight * jnp.roll(values, -1, 2)  10.2 us
    slice x4, local copies, waits for them, and re-layouts, from_symmetry(): jnp.roll(values, 1, 2)  5.88 us
    convert_element_type x1, other arithmetic, from_symmetry(): return values.reshape(rows_dev, cols_dev).astype(jnp.bfloat16)  4.71 us
    add x3, other arithmetic, strip_steps(): middle_weight * middle + eastward_weight * jnp.roll(middle, -1, 1)  4.09 us
  transfers between devices with their start and end apart: 10, of which 7 were waited for; matrix products, arithmetic and copies ran while one was open for 11% of the time, Pallas kernels for 0%

commit v1 on v0

v1 whole, which is shorter than its diff:
```python
import functools

import jax
import jax.numpy as jnp
from jax import lax
from jax.experimental import pallas as pl
from jax.experimental.pallas import tpu as pltpu
from jax.sharding import PartitionSpec as P

MESH = pl.DeviceIdType.MESH
F32 = jnp.float32
BF16 = jnp.bfloat16
STEPS = 3


def chunk_of(i):
    return jnp.where(i < 2, i + 3, jnp.where(i < 5, i - 2, i))


def put_weights(dst, span, first_lat, nlat, table, diffusivity, index):
    for step in range(STEPS):

        def one(place, carry, step=step):
            lat = first_lat + place
            inside = jnp.where((lat >= 0) & (lat < nlat), 1.0, 0.0).astype(F32)
            regime = index[step, jnp.clip(lat, 0, nlat - 1)]
            zonal, merid, diffuse = table[regime, 0], table[regime, 1], diffusivity[regime]
            zz, mm = 0.5 * zonal * zonal, 0.5 * merid * merid
            at = (step * span + place) * 5
            dst[at] = inside * (1.0 - zonal * zonal - merid * merid - 4.0 * diffuse)
            dst[at + 1] = inside * (zz - 0.5 * zonal + diffuse)
            dst[at + 2] = inside * (zz + 0.5 * zonal + diffuse)
            dst[at + 3] = inside * (mm - 0.5 * merid + diffuse)
            dst[at + 4] = inside * (mm + 0.5 * merid + diffuse)
            return carry

        lax.fori_loop(step + 1, span - 1 - step, one, 0)


def kernel(
    nlat, nrow, ncol,
    cov, noise, table, diffusivity, index,
    out, s_out,
    buf0, buf1, buf2, tt, sb, l2, r2, l1, r1, ob, w_row, w_col,
    load_sem, row_send, row_recv, one_send, one_recv, two_send, two_recv, out_sem, s_sem,
):
    strip, nlon, width = cov.shape
    row, col = lax.axis_index("row"), lax.axis_index("col")
    has_up, has_down = row > 0, row < nrow - 1
    has_left, has_right = col > 0, col < ncol - 1
    up, down = (lax.rem(row + nrow - 1, nrow), col), (lax.rem(row + 1, nrow), col)
    left, right = (row, lax.rem(col + ncol - 1, ncol)), (row, lax.rem(col + 1, ncol))
    span = strip + 2 * STEPS

    load = pltpu.make_async_copy(cov, buf0.at[pl.ds(STEPS, strip)], load_sem)
    load.start()

    barrier = pltpu.get_barrier_semaphore()
    count = 0
    for there, peer in ((has_up, up), (has_down, down), (has_left, left), (has_right, right)):

        @pl.when(there)
        def _(peer=peer):
            pl.semaphore_signal(barrier, inc=1, device_id=peer, device_id_type=MESH)

        count = count + jnp.where(there, 1, 0)

    put_weights(w_row, span, row * strip - STEPS, nlat, table, diffusivity, index)
    put_weights(w_col, 8, col * 2 - STEPS, nlat, table, diffusivity, index)

    @pl.when(jnp.logical_not(has_up))
    def _():
        buf0[pl.ds(0, STEPS)] = jnp.zeros((STEPS, nlon, width), F32)

    @pl.when(jnp.logical_not(has_down))
    def _():
        buf0[pl.ds(strip + STEPS, STEPS)] = jnp.zeros((STEPS, nlon, width), F32)

    @pl.when(jnp.logical_not(has_left))
    def _():
        l2[...] = jnp.zeros(l2.shape, BF16)
        l1[...] = jnp.zeros(l1.shape, BF16)

    @pl.when(jnp.logical_not(has_right))
    def _():
        r2[...] = jnp.zeros(r2.shape, BF16)
        r1[...] = jnp.zeros(r1.shape, BF16)

    pl.semaphore_wait(barrier, count)

    to_up = pltpu.make_async_remote_copy(
        src_ref=cov.at[pl.ds(0, STEPS)], dst_ref=buf0.at[pl.ds(strip + STEPS, STEPS)],
        send_sem=row_send.at[0], recv_sem=row_recv.at[0], device_id=up, device_id_type=MESH,
    )
    to_down = pltpu.make_async_remote_copy(
        src_ref=cov.at[pl.ds(strip - STEPS, STEPS)], dst_ref=buf0.at[pl.ds(0, STEPS)],
        send_sem=row_send.at[1], recv_sem=row_recv.at[1], device_id=down, device_id_type=MESH,
    )

    @pl.when(has_up)
    def _():
        to_up.start()

    @pl.when(has_down)
    def _():
        to_down.start()

    def rows_step(src, dst, step, first, last, base):
        def one(place, carry):
            at = (step * span + place) * 5
            mid, east, west, north, south = (w_row[at + n] for n in range(5))
            for half in range(width // 128):
                lanes = pl.ds(half * 128, 128)
                value = src[place, :, lanes]
                value = (
                    mid * value
                    + east * pltpu.roll(value, nlon - 1, 0)
                    + west * pltpu.roll(value, 1, 0)
                    + north * src[place + 1, :, lanes]
                    + south * src[place - 1, :, lanes]
                )
                dst[place - base, :, lanes] = value
                if step == STEPS - 1:
                    sb[place - base, :, lanes] = value.astype(BF16)
            return carry

        lax.fori_loop(first, last, one, 0)

    def first_message(i, side):
        lat = chunk_of(i)
        return pltpu.make_async_remote_copy(
            src_ref=sb.at[lat], dst_ref=(l2, r2)[side].at[lat],
            send_sem=one_send.at[side, i], recv_sem=one_recv.at[side, i],
            device_id=(right, left)[side], device_id_type=MESH,
        )

    def second_message(i, side):
        lat = chunk_of(i)
        lanes = (pl.ds(128, 128), pl.ds(0, 128))[side]
        return pltpu.make_async_remote_copy(
            src_ref=(l2, r2)[side].at[lat, :, lanes], dst_ref=(l1, r1)[side].at[lat],
            send_sem=two_send.at[side, i], recv_sem=two_recv.at[side, i],
            device_id=(right, left)[side], device_id_type=MESH,
        )

    def store_s(i):
        lat = chunk_of(i)
        return pltpu.make_async_copy(sb.at[lat], s_out.at[lat], s_sem.at[i])

    def store_out(i):
        lat = chunk_of(i)
        return pltpu.make_async_copy(ob.at[lat], out.at[lat], out_sem.at[i])

    def send_first(start, stop):
        def one(i, carry):
            @pl.when(has_right)
            def _():
                first_message(i, 0).start()

            @pl.when(has_left)
            def _():
                first_message(i, 1).start()

            store_s(i).start()
            return carry

        lax.fori_loop(start, stop, one, 0)

    load.wait()
    rows_step(buf0, buf1, 0, 4, 10, 0)
    rows_step(buf1, buf2, 1, 5, 9, 0)
    rows_step(buf2, tt, 2, 6, 8, STEPS)
    send_first(0, 2)

    @pl.when(has_up)
    def _():
        to_down.wait_recv()

    rows_step(buf0, buf1, 0, 1, 4, 0)
    rows_step(buf1, buf2, 1, 2, 5, 0)
    rows_step(buf2, tt, 2, 3, 6, STEPS)
    send_first(2, 5)

    @pl.when(has_down)
    def _():
        to_up.wait_recv()

    rows_step(buf0, buf1, 0, 10, 13, 0)
    rows_step(buf1, buf2, 1, 9, 12, 0)
    rows_step(buf2, tt, 2, 8, 11, STEPS)
    send_first(5, 8)

    def pass_on(i):
        @pl.when(has_left)
        def _():
            first_message(i, 0).wait_recv()

            @pl.when(has_right)
            def _():
                second_message(i, 0).start()

        @pl.when(has_right)
        def _():
            first_message(i, 1).wait_recv()

            @pl.when(has_left)
            def _():
                second_message(i, 1).start()

    def columns(i):
        lat = chunk_of(i)

        @pl.when(col > 1)
        def _():
            second_message(i, 0).wait_recv()

        @pl.when(col < ncol - 2)
        def _():
            second_message(i, 1).wait_recv()

        def one(q, carry):
            rows = pl.ds(pl.multiple_of(q * 16, 16), 16)
            v = [
                l1[lat, rows, :],
                l2[lat, rows, 0:128],
                l2[lat, rows, 128:256],
                tt[lat, rows, 0:128],
                tt[lat, rows, 128:256],
                r2[lat, rows, 0:128],
                r2[lat, rows, 128:256],
                r1[lat, rows, :],
            ]
            v = [x.astype(F32) for x in v]
            for step in range(STEPS):
                fresh = []
                for n in range(1, len(v) - 1):
                    at = (step * 8 + n + step) * 5
                    mid, east, west, north, south = (w_col[at + m] for m in range(5))
                    fresh.append(
                        mid * v[n]
                        + east * pltpu.roll(v[n], 127, 1)
                        + west * pltpu.roll(v[n], 1, 1)
                        + north * v[n + 1]
                        + south * v[n - 1]
                    )
                v = fresh
            ob[lat, rows, 0:128] = v[0]
            ob[lat, rows, 128:256] = v[1]
            return carry

        lax.fori_loop(0, nlon // 16, one, 0)
        for half in range(2):

            @pl.when(row * strip + lat == col * 2 + half)
            def _(half=half):
                lanes = pl.ds(half * 128, 128)
                own = lax.broadcasted_iota(jnp.int32, (128, 128), 0) == lax.broadcasted_iota(
                    jnp.int32, (128, 128), 1
                )
                line = noise[pl.ds(lat, 1), :]
                ob[lat, :, lanes] = ob[lat, :, lanes] + jnp.where(own, line, 0.0)

        store_out(i).start()

    pass_on(0)

    def turn(i, carry):
        @pl.when(i < strip)
        def _():
            pass_on(i)

        columns(i - 1)
        return carry

    lax.fori_loop(1, strip + 1, turn, 0)

    def finish(i, carry):
        store_s(i).wait()
        store_out(i).wait()

        @pl.when(has_right)
        def _():
            first_message(i, 0).wait_send()

        @pl.when(has_left)
        def _():
            first_message(i, 1).wait_send()

        @pl.when(has_left & has_right)
        def _():
            second_message(i, 0).wait_send()
            second_message(i, 1).wait_send()

        return carry

    lax.fori_loop(0, strip, finish, 0)

    @pl.when(has_up)
    def _():
        to_up.wait_send()

    @pl.when(has_down)
    def _():
        to_down.wait_send()


def solution(mesh):
    nrow, ncol = mesh.shape["row"], mesh.shape["col"]

    def body(covariance, noise_var, wind_table, diffusivity, wind_index):
        rows_dev, cols_dev = covariance.shape
        strip, nlon = noise_var.shape
        nlat = wind_index.shape[1]
        block = (strip, nlon, cols_dev)
        half = (strip, nlon, nlon)
        span = (strip + 2 * STEPS, nlon, cols_dev)
        anywhere = pl.BlockSpec(memory_space=pl.ANY)
        scalars = pl.BlockSpec(memory_space=pltpu.SMEM)
        out, s = pl.pallas_call(
            functools.partial(kernel, nlat, nrow, ncol),
            out_shape=(jax.ShapeDtypeStruct(block, F32), jax.ShapeDtypeStruct(block, BF16)),
            in_specs=[anywhere, pl.BlockSpec(memory_space=pltpu.VMEM), scalars, scalars, scalars],
            out_specs=(anywhere, anywhere),
            scratch_shapes=[
                pltpu.VMEM(span, F32),
                pltpu.VMEM(span, F32),
                pltpu.VMEM(span, F32),
                pltpu.VMEM(block, F32),
                pltpu.VMEM(block, BF16),
                pltpu.VMEM(block, BF16),
                pltpu.VMEM(block, BF16),
                pltpu.VMEM(half, BF16),
                pltpu.VMEM(half, BF16),
                pltpu.VMEM(block, F32),
                pltpu.SMEM((STEPS * (strip + 2 * STEPS) * 5,), F32),
                pltpu.SMEM((STEPS * 8 * 5,), F32),
                pltpu.SemaphoreType.DMA,
                pltpu.SemaphoreType.DMA((2,)),
                pltpu.SemaphoreType.DMA((2,)),
                pltpu.SemaphoreType.DMA((2, strip)),
                pltpu.SemaphoreType.DMA((2, strip)),
                pltpu.SemaphoreType.DMA((2, strip)),
                pltpu.SemaphoreType.DMA((2, strip)),
                pltpu.SemaphoreType.DMA((strip,)),
                pltpu.SemaphoreType.DMA((strip,)),
            ],
            compiler_params=pltpu.CompilerParams(collective_id=0, has_side_effects=True),
        )(covariance.reshape(block), noise_var, wind_table, diffusivity, wind_index)
        return out.reshape(rows_dev, cols_dev), s.reshape(rows_dev, cols_dev)

    in_specs = (P("row", "col"), P("row", None), P(), P(), P())
    out_specs = (P("row", "col"), P("row", "col"))
    return jax.shard_map(body, mesh=mesh, in_specs=in_specs, out_specs=out_specs, check_vma=False)
```

time: 142 us -> 80.6 us (0.57)
  the two profiles are of different devices: /device:TPU:129 before, /device:TPU:62 now
where the time goes in v1:
time: 80.6 us; the launch traced here: 80.4 us
  Pallas kernels  75.3 us (93%)
  local copies, waits for them, and re-layouts  4.47 us (6%)
    pallas_call x1, Pallas kernels, body(): pl.pallas_call(functools.partial(kernel, nlat, nrow, ncol), out_shape=(ja...  75.3 us
    unnamed x7, local copies, waits for them, and re-layouts  4.47 us

profile of v1, /device:TPU:62, one launch (start us, length us, event | category | flops | bytes accessed | tf_op | source)
XLA Modules:
  0.0 80.4 jit_solution(1651204542272373721)
XLA Ops:
  0.6 0.0 copy-start.1
  0.6 0.7 copy-done.1
  1.3 0.7 copy.7.table
  2.0 75.3 %shard_map.68 = (f32[8,128,256]{2,1,0:T(8,128)}, bf16[8,128,256]{2,1,0:T(8,128)(2,1)}) custom-call(f32[8,128,256]{2,1,0:T(8,128)} %bitcast.3, f32[8,128]{1,0:T(8,128)} %noise.1, f32[16,2]{1,0:T(8,128)} %copy.7.table, f32[16]{0:T(128)} %diffusivity.1, s32[3,64]{1,0:T(4,128)} %index.1), custom_call_target="tpu_custom_call" | custom-call | tf_op jit(solution)/shard_map/pallas_call | solution.py:319
  77.3 0.0 copy-start
  77.3 2.3 %copy.10 = f32[1024,256]{1,0:T(8,128)} copy(f32[1024,256]{1,0:T(8,128)} %bitcast.4) | data formatting | bytes 2097152
  79.6 0.0 copy-done
  79.6 0.8 copy.11
Async XLA Ops:
  0.6 0.7 copy-start.1
  77.3 2.3 %copy-start = (bf16[8,128,256]{2,1,0:T(8,128)(2,1)S(1)}, bf16[8,128,256]{2,1,0:T(8,128)(2,1)}, u32[]{:S(2)}) copy-start(bf16[8,128,256]{2,1,0:T(8,128)(2,1)} %get-tuple-element.5) | copy-start | bytes 1572868

commit v2 on v1

--- a/solution.py
+++ b/solution.py
@@ -11,6 +11,7 @@
 F32 = jnp.float32
 BF16 = jnp.bfloat16
 STEPS = 3
+AHEAD = 3
 
 
 def chunk_of(i):
@@ -24,7 +25,7 @@
             lat = first_lat + place
             inside = jnp.where((lat >= 0) & (lat < nlat), 1.0, 0.0).astype(F32)
             regime = index[step, jnp.clip(lat, 0, nlat - 1)]
-            zonal, merid, diffuse = table[regime, 0], table[regime, 1], diffusivity[regime]
+            zonal, merid, diffuse = table[0, regime], table[1, regime], diffusivity[regime]
             zz, mm = 0.5 * zonal * zonal, 0.5 * merid * merid
             at = (step * span + place) * 5
             dst[at] = inside * (1.0 - zonal * zonal - merid * merid - 4.0 * diffuse)
@@ -40,9 +41,9 @@
 def kernel(
     nlat, nrow, ncol,
     cov, noise, table, diffusivity, index,
-    out, s_out,
-    buf0, buf1, buf2, tt, sb, l2, r2, l1, r1, ob, w_row, w_col,
-    load_sem, row_send, row_recv, one_send, one_recv, two_send, two_recv, out_sem, s_sem,
+    ob, sb,
+    buf0, buf1, buf2, low, l2, r2, far, held, w_high, w_low, w_row, w_col,
+    load_sem, row_send, row_recv, one_send, one_recv, two_send, two_recv, held_send, held_recv,
 ):
     strip, nlon, width = cov.shape
     row, col = lax.axis_index("row"), lax.axis_index("col")
@@ -52,11 +53,30 @@
     left, right = (row, lax.rem(col + ncol - 1, ncol)), (row, lax.rem(col + 1, ncol))
     span = strip + 2 * STEPS
 
+    edge = ncol // 2 - 1
+    near_relay = (col == edge - 3) | (col == edge + 4)
+    far_relay = (col == 0) | (col == ncol - 1)
+    relays = near_relay | far_relay
+    at_edge = (col == edge) | (col == edge + 1)
+    lower = col <= edge
+    relay_from = jnp.where(lower, edge, edge + 1)
+    relay_to = jnp.where(lower, edge + 1, edge)
+
     load = pltpu.make_async_copy(cov, buf0.at[pl.ds(STEPS, strip)], load_sem)
     load.start()
 
     barrier = pltpu.get_barrier_semaphore()
-    count = 0
+
+    @pl.when(at_edge)
+    def _():
+        for peer in (jnp.where(lower, edge + 4, 0), jnp.where(lower, ncol - 1, edge - 3)):
+            pl.semaphore_signal(barrier, inc=1, device_id=(row, peer), device_id_type=MESH)
+
+    @pl.when(relays)
+    def _():
+        pl.semaphore_signal(barrier, inc=1, device_id=(row, relay_from), device_id_type=MESH)
+
+    count = jnp.where(at_edge, 2, 0) + jnp.where(relays, 1, 0)
     for there, peer in ((has_up, up), (has_down, down), (has_left, left), (has_right, right)):
 
         @pl.when(there)
@@ -79,12 +99,43 @@
     @pl.when(jnp.logical_not(has_left))
     def _():
         l2[...] = jnp.zeros(l2.shape, BF16)
-        l1[...] = jnp.zeros(l1.shape, BF16)
 
     @pl.when(jnp.logical_not(has_right))
     def _():
         r2[...] = jnp.zeros(r2.shape, BF16)
-        r1[...] = jnp.zeros(r1.shape, BF16)
+
+    @pl.when(col <= 1)
+    def _():
+        far[:, :, 0:128] = jnp.zeros((strip, nlon, 128), BF16)
+
+    @pl.when(col >= ncol - 2)
+    def _():
+        far[:, :, 128:256] = jnp.zeros((strip, nlon, 128), BF16)
+
+    sub = lax.broadcasted_iota(jnp.int32, (8, 128), 0)
+    middle = lax.broadcasted_iota(jnp.int32, (8, 128), 1) == 64
+    v = [jnp.where((sub == n) & middle, 1.0, 0.0).astype(F32) for n in range(8)]
+    for step in range(STEPS):
+        fresh = []
+        for n in range(1, len(v) - 1):
+            at = (step * 8 + n + step) * 5
+            mid, east, west, north, south = (w_col[at + m] for m in range(5))
+            fresh.append(
+                mid * v[n]
+                + east * pltpu.roll(v[n], 127, 1)
+                + west * pltpu.roll(v[n], 1, 1)
+                + north * v[n + 1]
+                + south * v[n - 1]
+            )
+        v = fresh
+    for place, lat in enumerate((0, 7, 1, 2, 3, 4, 5, 6)):
+        for half in range(2):
+            line = jnp.broadcast_to(v[half][lat : lat + 1, :], (128, 128))
+            block = pltpu.roll(line, 64, 1, stride=1, stride_axis=0)
+            rows, lanes = pl.ds((place % 2) * 128, 128), pl.ds(half * 128, 128)
+            high = block.astype(BF16)
+            w_high[place // 2, rows, lanes] = high
+            w_low[place // 2, rows, lanes] = (block - high.astype(F32)).astype(BF16)
 
     pl.semaphore_wait(barrier, count)
 
@@ -119,9 +170,12 @@
                     + north * src[place + 1, :, lanes]
                     + south * src[place - 1, :, lanes]
                 )
-                dst[place - base, :, lanes] = value
-                if step == STEPS - 1:
-                    sb[place - base, :, lanes] = value.astype(BF16)
+                if step < STEPS - 1:
+                    dst[place - base, :, lanes] = value
+                else:
+                    high = value.astype(BF16)
+                    sb[place - base, :, lanes] = high
+                    dst[place - base, :, lanes] = (value - high.astype(F32)).astype(BF16)
             return carry
 
         lax.fori_loop(first, last, one, 0)
@@ -134,34 +188,50 @@
             device_id=(right, left)[side], device_id_type=MESH,
         )
 
+    def to_relay(i, side):
+        near, away = ((edge - 3, 0), (edge + 4, ncol - 1))[side]
+        return pltpu.make_async_remote_copy(
+            src_ref=sb.at[chunk_of(i)], dst_ref=held.at[i // 2],
+            send_sem=one_send.at[side, i], recv_sem=held_recv.at[i // 2],
+            device_id=(row, jnp.where(lax.rem(i, 2) == 0, near, away)), device_id_type=MESH,
+        )
+
+    def from_relay(j, side):
+        i = 2 * j + jnp.where(near_relay, 0, 1)
+        return pltpu.make_async_remote_copy(
+            src_ref=held.at[j], dst_ref=(l2, r2)[side].at[chunk_of(i)],
+            send_sem=held_send.at[j], recv_sem=one_recv.at[side, i],
+            device_id=(row, relay_to), device_id_type=MESH,
+        )
+
     def second_message(i, side):
         lat = chunk_of(i)
         lanes = (pl.ds(128, 128), pl.ds(0, 128))[side]
         return pltpu.make_async_remote_copy(
-            src_ref=(l2, r2)[side].at[lat, :, lanes], dst_ref=(l1, r1)[side].at[lat],
+            src_ref=(l2, r2)[side].at[lat, :, lanes],
+            dst_ref=far.at[lat, :, pl.ds(side * 128, 128)],
             send_sem=two_send.at[side, i], recv_sem=two_recv.at[side, i],
             device_id=(right, left)[side], device_id_type=MESH,
         )
 
-    def store_s(i):
-        lat = chunk_of(i)
-        return pltpu.make_async_copy(sb.at[lat], s_out.at[lat], s_sem.at[i])
-
-    def store_out(i):
-        lat = chunk_of(i)
-        return pltpu.make_async_copy(ob.at[lat], out.at[lat], out_sem.at[i])
-
     def send_first(start, stop):
         def one(i, carry):
-            @pl.when(has_right)
+            @pl.when(has_right & (col != edge))
             def _():
                 first_message(i, 0).start()
 
-            @pl.when(has_left)
+            @pl.when(col == edge)
+            def _():
+                to_relay(i, 0).start()
+
+            @pl.when(has_left & (col != edge + 1))
             def _():
                 first_message(i, 1).start()
 
-            store_s(i).start()
+            @pl.when(col == edge + 1)
+            def _():
+                to_relay(i, 1).start()
+
             return carry
 
         lax.fori_loop(start, stop, one, 0)
@@ -169,7 +239,7 @@
     load.wait()
     rows_step(buf0, buf1, 0, 4, 10, 0)
     rows_step(buf1, buf2, 1, 5, 9, 0)
-    rows_step(buf2, tt, 2, 6, 8, STEPS)
+    rows_step(buf2, low, 2, 6, 8, STEPS)
     send_first(0, 2)
 
     @pl.when(has_up)
@@ -178,7 +248,7 @@
 
     rows_step(buf0, buf1, 0, 1, 4, 0)
     rows_step(buf1, buf2, 1, 2, 5, 0)
-    rows_step(buf2, tt, 2, 3, 6, STEPS)
+    rows_step(buf2, low, 2, 3, 6, STEPS)
     send_first(2, 5)
 
     @pl.when(has_down)
@@ -187,7 +257,7 @@
 
     rows_step(buf0, buf1, 0, 10, 13, 0)
     rows_step(buf1, buf2, 1, 9, 12, 0)
-    rows_step(buf2, tt, 2, 8, 11, STEPS)
+    rows_step(buf2, low, 2, 8, 11, STEPS)
     send_first(5, 8)
 
     def pass_on(i):
@@ -218,37 +288,14 @@
         def _():
             second_message(i, 1).wait_recv()
 
-        def one(q, carry):
-            rows = pl.ds(pl.multiple_of(q * 16, 16), 16)
-            v = [
-                l1[lat, rows, :],
-                l2[lat, rows, 0:128],
-                l2[lat, rows, 128:256],
-                tt[lat, rows, 0:128],
-                tt[lat, rows, 128:256],
-                r2[lat, rows, 0:128],
-                r2[lat, rows, 128:256],
-                r1[lat, rows, :],
-            ]
-            v = [x.astype(F32) for x in v]
-            for step in range(STEPS):
-                fresh = []
-                for n in range(1, len(v) - 1):
-                    at = (step * 8 + n + step) * 5
-                    mid, east, west, north, south = (w_col[at + m] for m in range(5))
-                    fresh.append(
-                        mid * v[n]
-                        + east * pltpu.roll(v[n], 127, 1)
-                        + west * pltpu.roll(v[n], 1, 1)
-                        + north * v[n + 1]
-                        + south * v[n - 1]
-                    )
-                v = fresh
-            ob[lat, rows, 0:128] = v[0]
-            ob[lat, rows, 128:256] = v[1]
-            return carry
-
-        lax.fori_loop(0, nlon // 16, one, 0)
+        def dot(x, w):
+            return jnp.dot(x, w, preferred_element_type=F32)
+
+        total = dot(low[lat], w_high[2])
+        for place, ref in enumerate((far, l2, sb, r2)):
+            x = ref[lat]
+            total = total + dot(x, w_high[place]) + dot(x, w_low[place])
+        ob[lat] = total
         for half in range(2):
 
             @pl.when(row * strip + lat == col * 2 + half)
@@ -260,24 +307,34 @@
                 line = noise[pl.ds(lat, 1), :]
                 ob[lat, :, lanes] = ob[lat, :, lanes] + jnp.where(own, line, 0.0)
 
-        store_out(i).start()
-
-    pass_on(0)
-
     def turn(i, carry):
         @pl.when(i < strip)
         def _():
             pass_on(i)
 
-        columns(i - 1)
+        @pl.when(relays & (i < strip) & (lax.rem(i, 2) == 1))
+        def _():
+            j = i // 2
+
+            @pl.when(lower)
+            def _():
+                to_relay(2 * j, 0).wait_recv()
+                from_relay(j, 0).start()
+
+            @pl.when(jnp.logical_not(lower))
+            def _():
+                to_relay(2 * j, 1).wait_recv()
+                from_relay(j, 1).start()
+
+        @pl.when(i >= AHEAD)
+        def _():
+            columns(i - AHEAD)
+
         return carry
 
-    lax.fori_loop(1, strip + 1, turn, 0)
+    lax.fori_loop(0, strip + AHEAD, turn, 0)
 
     def finish(i, carry):
-        store_s(i).wait()
-        store_out(i).wait()
-
         @pl.when(has_right)
         def _():
             first_message(i, 0).wait_send()
@@ -294,6 +351,12 @@
         return carry
 
     lax.fori_loop(0, strip, finish, 0)
+
+    @pl.when(relays)
+    def _():
+        for j in range(strip // 2):
+            from_relay(j, 0).wait_send()
+
 
     @pl.when(has_up)
     def _():
@@ -312,26 +375,25 @@
         strip, nlon = noise_var.shape
         nlat = wind_index.shape[1]
         block = (strip, nlon, cols_dev)
-        half = (strip, nlon, nlon)
         span = (strip + 2 * STEPS, nlon, cols_dev)
-        anywhere = pl.BlockSpec(memory_space=pl.ANY)
+        anywhere = pl.BlockSpec(memory_space=pltpu.HBM)
         scalars = pl.BlockSpec(memory_space=pltpu.SMEM)
         out, s = pl.pallas_call(
             functools.partial(kernel, nlat, nrow, ncol),
             out_shape=(jax.ShapeDtypeStruct(block, F32), jax.ShapeDtypeStruct(block, BF16)),
             in_specs=[anywhere, pl.BlockSpec(memory_space=pltpu.VMEM), scalars, scalars, scalars],
-            out_specs=(anywhere, anywhere),
+            out_specs=(pl.BlockSpec(memory_space=pltpu.VMEM),) * 2,
             scratch_shapes=[
                 pltpu.VMEM(span, F32),
                 pltpu.VMEM(span, F32),
                 pltpu.VMEM(span, F32),
-                pltpu.VMEM(block, F32),
                 pltpu.VMEM(block, BF16),
                 pltpu.VMEM(block, BF16),
                 pltpu.VMEM(block, BF16),
-                pltpu.VMEM(half, BF16),
-                pltpu.VMEM(half, BF16),
-                pltpu.VMEM(block, F32),
+                pltpu.VMEM(block, BF16),
+                pltpu.VMEM((strip // 2, nlon, cols_dev), BF16),
+                pltpu.VMEM((4, 256, 256), BF16),
+                pltpu.VMEM((4, 256, 256), BF16),
                 pltpu.SMEM((STEPS * (strip + 2 * STEPS) * 5,), F32),
                 pltpu.SMEM((STEPS * 8 * 5,), F32),
                 pltpu.SemaphoreType.DMA,
@@ -341,11 +403,11 @@
                 pltpu.SemaphoreType.DMA((2, strip)),
                 pltpu.SemaphoreType.DMA((2, strip)),
                 pltpu.SemaphoreType.DMA((2, strip)),
-                pltpu.SemaphoreType.DMA((strip,)),
-                pltpu.SemaphoreType.DMA((strip,)),
+                pltpu.SemaphoreType.DMA((strip // 2,)),
+                pltpu.SemaphoreType.DMA((strip // 2,)),
             ],
-            compiler_params=pltpu.CompilerParams(collective_id=0, has_side_effects=True),
-        )(covariance.reshape(block), noise_var, wind_table, diffusivity, wind_index)
+            compiler_params=pltpu.CompilerParams(collective_id=0, has_side_effects=True, vmem_limit_bytes=14 << 20),
+        )(covariance.reshape(block), noise_var, wind_table.T, diffusivity, wind_index)
         return out.reshape(rows_dev, cols_dev), s.reshape(rows_dev, cols_dev)
 
     in_specs = (P("row", "col"), P("row", None), P(), P(), P())

time: 80.6 us -> 60.3 us (0.75)
  Pallas kernels: 75.3 us -> 55.1 us
    pallas_call x1, Pallas kernels: 75.3 us -> 55.1 us  [body(): pl.pallas_call(functools.partial(kernel, nlat, nrow, ncol), out_shape=(ja...]
    unnamed x7 -> x12, local copies, waits for them, and re-layouts: 4.47 us -> 4.35 us
where the time goes in v2:
time: 60.3 us; the launch traced here: 60.2 us
  Pallas kernels  55.1 us (91%)
  local copies, waits for them, and re-layouts  4.35 us (7%)
  between operations  0.67 us (1%)
    pallas_call x1, Pallas kernels, body(): pl.pallas_call(functools.partial(kernel, nlat, nrow, ncol), out_shape=(ja...  55.1 us
    unnamed x12, local copies, waits for them, and re-layouts  4.35 us

profile of v2, /device:TPU:62, one launch (start us, length us, event | category | flops | bytes accessed | tf_op | source)
XLA Modules:
  0.0 60.2 jit_solution(12561947562369842699)
XLA Ops:
  0.6 0.0 copy-start.2
  0.6 0.0 copy-start.3
  0.7 0.0 copy-start.4
  0.7 0.7 %copy-done.2 = s32[3,64]{1,0:T(4,128)S(1)} copy-done((s32[3,64]{1,0:T(4,128)S(1)}, s32[3,64]{1,0:T(4,128)}, u32[]{:S(2)}) %copy-start.2) | copy-done | bytes 792
  1.3 0.0 copy-done.3
  1.3 0.0 copy-done.4
  1.3 0.0 copy-start
  1.3 1.2 %copy-done = f32[1024,256]{1,0:T(8,128)S(1)} copy-done((f32[1024,256]{1,0:T(8,128)S(1)}, f32[1024,256]{1,0:T(8,128)}, u32[]{:S(2)}) %copy-start) | copy-done | bytes 1048600
  2.6 0.0 copy-start.1
  2.6 0.7 %copy-done.1 = f32[8,128]{1,0:T(8,128)S(1)} copy-done((f32[8,128]{1,0:T(8,128)S(1)}, f32[8,128]{1,0:T(8,128)}, u32[]{:S(2)}) %copy-start.1) | copy-done | bytes 4120
  3.2 55.1 %shard_map.68 = (f32[8,128,256]{2,1,0:T(8,128)S(1)}, bf16[8,128,256]{2,1,0:T(8,128)(2,1)S(1)}) custom-call(f32[8,128,256]{2,1,0:T(8,128)S(1)} %bitcast.4, f32[8,128]{1,0:T(8,128)S(1)} %copy-done.1, f32[2,16]{1,0:T(2,128)S(1)} %bitcast.7, f32[16]{0:T(128)S(1)} %copy-done.4, s32[3,64]{1,0:T(4,128)S(1)} %copy-done.2), custom_call_target="tpu_custom_call" | custom-call | tf_op jit(solution)/shard_map/pallas_call | solution.py:381
  58.4 1.0 %copy.9 = f32[1024,256]{1,0:T(8,128)} copy(f32[1024,256]{1,0:T(8,128)S(1)} %bitcast.5) | data formatting | bytes 2097152
  59.4 0.8 %copy.10 = bf16[1024,256]{1,0:T(8,128)(2,1)} copy(bf16[1024,256]{1,0:T(8,128)(2,1)S(1)} %bitcast.6) | data formatting | bytes 1048576
Async XLA Ops:
  0.6 0.7 %copy-start.2 = (s32[3,64]{1,0:T(4,128)S(1)}, s32[3,64]{1,0:T(4,128)}, u32[]{:S(2)}) copy-start(s32[3,64]{1,0:T(4,128)} %index.1) | copy-start | bytes 2308
  0.6 0.7 %copy-start.3 = (f32[16,2]{0,1:T(2,128)S(1)}, f32[16,2]{0,1:T(2,128)}, u32[]{:S(2)}) copy-start(f32[16,2]{0,1:T(2,128)} %param.7) | copy-start | bytes 388
  0.7 0.7 %copy-start.4 = (f32[16]{0:T(128)S(1)}, f32[16]{0:T(128)}, u32[]{:S(2)}) copy-start(f32[16]{0:T(128)} %diffusivity.1) | copy-start | bytes 196
  1.3 1.2 %copy-start = (f32[1024,256]{1,0:T(8,128)S(1)}, f32[1024,256]{1,0:T(8,128)}, u32[]{:S(2)}) copy-start(f32[1024,256]{1,0:T(8,128)} %param.5) | copy-start | bytes 3145732
  2.6 0.7 %copy-start.1 = (f32[8,128]{1,0:T(8,128)S(1)}, f32[8,128]{1,0:T(8,128)}, u32[]{:S(2)}) copy-start(f32[8,128]{1,0:T(8,128)} %noise.1) | copy-start | bytes 12292

commit v3 on v2

--- a/solution.py
+++ b/solution.py
@@ -11,11 +11,11 @@
 F32 = jnp.float32
 BF16 = jnp.bfloat16
 STEPS = 3
-AHEAD = 3
 
 
 def chunk_of(i):
-    return jnp.where(i < 2, i + 3, jnp.where(i < 5, i - 2, i))
+    even = lax.rem(lax.axis_index("row"), 2) == 0
+    return jnp.where(i < 2, i + 3, jnp.where(even, jnp.where(i < 5, i + 3, i - 5), jnp.where(i < 5, i - 2, i)))
 
 
 def put_weights(dst, span, first_lat, nlat, table, diffusivity, index):
@@ -42,20 +42,22 @@
     nlat, nrow, ncol,
     cov, noise, table, diffusivity, index,
     ob, sb,
-    buf0, buf1, buf2, low, l2, r2, far, held, w_high, w_low, w_row, w_col,
-    load_sem, row_send, row_recv, one_send, one_recv, two_send, two_recv, held_send, held_recv,
+    buf0, buf1, buf2, low, l2, r2, far, held, held_far, w_high, w_low, w_row, w_col,
+    load_sem, row_send, row_recv, one_send, one_recv, two_send, two_recv, held_send, held_recv, far_send, far_recv,
 ):
     strip, nlon, width = cov.shape
     row, col = lax.axis_index("row"), lax.axis_index("col")
     has_up, has_down = row > 0, row < nrow - 1
     has_left, has_right = col > 0, col < ncol - 1
+    next_left, next_right = has_left & (col != ncol // 2), has_right & (col != ncol // 2 - 1)
     up, down = (lax.rem(row + nrow - 1, nrow), col), (lax.rem(row + 1, nrow), col)
     left, right = (row, lax.rem(col + ncol - 1, ncol)), (row, lax.rem(col + 1, ncol))
     span = strip + 2 * STEPS
 
     edge = ncol // 2 - 1
-    near_relay = (col == edge - 3) | (col == edge + 4)
+    near_relay = (col == 3) | (col == ncol - 4)
     far_relay = (col == 0) | (col == ncol - 1)
+    pass_relay = (col == 7) | (col == ncol - 8)
     relays = near_relay | far_relay
     at_edge = (col == edge) | (col == edge + 1)
     lower = col <= edge
@@ -69,15 +71,19 @@
 
     @pl.when(at_edge)
     def _():
-        for peer in (jnp.where(lower, edge + 4, 0), jnp.where(lower, ncol - 1, edge - 3)):
+        for peer in (
+            jnp.where(lower, ncol - 4, 0),
+            jnp.where(lower, ncol - 1, 3),
+            jnp.where(lower, ncol - 8, 7),
+        ):
             pl.semaphore_signal(barrier, inc=1, device_id=(row, peer), device_id_type=MESH)
 
-    @pl.when(relays)
+    @pl.when(relays | pass_relay)
     def _():
         pl.semaphore_signal(barrier, inc=1, device_id=(row, relay_from), device_id_type=MESH)
 
-    count = jnp.where(at_edge, 2, 0) + jnp.where(relays, 1, 0)
-    for there, peer in ((has_up, up), (has_down, down), (has_left, left), (has_right, right)):
+    count = jnp.where(at_edge, 3, 0) + jnp.where(relays | pass_relay, 1, 0)
+    for there, peer in ((has_up, up), (has_down, down), (next_left, left), (next_right, right)):
 
         @pl.when(there)
         def _(peer=peer):
@@ -189,7 +195,7 @@
         )
 
     def to_relay(i, side):
-        near, away = ((edge - 3, 0), (edge + 4, ncol - 1))[side]
+        near, away = ((3, 0), (ncol - 4, ncol - 1))[side]
         return pltpu.make_async_remote_copy(
             src_ref=sb.at[chunk_of(i)], dst_ref=held.at[i // 2],
             send_sem=one_send.at[side, i], recv_sem=held_recv.at[i // 2],
@@ -242,40 +248,56 @@
     rows_step(buf2, low, 2, 6, 8, STEPS)
     send_first(0, 2)
 
-    @pl.when(has_up)
-    def _():
-        to_down.wait_recv()
-
-    rows_step(buf0, buf1, 0, 1, 4, 0)
-    rows_step(buf1, buf2, 1, 2, 5, 0)
-    rows_step(buf2, low, 2, 3, 6, STEPS)
+    def end_rows(bottom):
+        @pl.when(jnp.logical_not(bottom) & has_up)
+        def _():
+            to_down.wait_recv()
+
+        @pl.when(bottom & has_down)
+        def _():
+            to_up.wait_recv()
+
+        for src, dst, step, top_first, bottom_first, base in (
+            (buf0, buf1, 0, 1, strip + 2, 0),
+            (buf1, buf2, 1, 2, strip + 1, 0),
+            (buf2, low, 2, 3, strip, STEPS),
+        ):
+            first = jnp.where(bottom, bottom_first, top_first)
+            rows_step(src, dst, step, first, first + STEPS, base)
+
+    even = lax.rem(row, 2) == 0
+    end_rows(even)
     send_first(2, 5)
-
-    @pl.when(has_down)
-    def _():
-        to_up.wait_recv()
-
-    rows_step(buf0, buf1, 0, 10, 13, 0)
-    rows_step(buf1, buf2, 1, 9, 12, 0)
-    rows_step(buf2, low, 2, 8, 11, STEPS)
+    end_rows(jnp.logical_not(even))
     send_first(5, 8)
 
-    def pass_on(i):
-        @pl.when(has_left)
-        def _():
-            first_message(i, 0).wait_recv()
-
-            @pl.when(has_right)
-            def _():
-                second_message(i, 0).start()
-
-        @pl.when(has_right)
-        def _():
-            first_message(i, 1).wait_recv()
-
-            @pl.when(has_left)
-            def _():
-                second_message(i, 1).start()
+    def pass_to_relay(i, side):
+        lanes = (pl.ds(128, 128), pl.ds(0, 128))[side]
+        return pltpu.make_async_remote_copy(
+            src_ref=(l2, r2)[side].at[chunk_of(i), :, lanes], dst_ref=held_far.at[i],
+            send_sem=two_send.at[side, i], recv_sem=far_recv.at[i],
+            device_id=(row, (7, ncol - 8)[side]), device_id_type=MESH,
+        )
+
+    def pass_from_relay(i, side):
+        return pltpu.make_async_remote_copy(
+            src_ref=held_far.at[i], dst_ref=far.at[chunk_of(i), :, pl.ds(side * 128, 128)],
+            send_sem=far_send.at[i], recv_sem=two_recv.at[side, i],
+            device_id=(row, relay_to), device_id_type=MESH,
+        )
+
+    def pass_on(i, side, there, onward):
+        @pl.when(there)
+        def _():
+            first_message(i, side).wait_recv()
+
+            @pl.when(onward)
+            def _():
+                second_message(i, side).start()
+
+            @pl.when(col == edge + side)
+            def _():
+                pass_to_relay(i, side).start()
 
     def columns(i):
         lat = chunk_of(i)
@@ -308,31 +330,39 @@
                 ob[lat, :, lanes] = ob[lat, :, lanes] + jnp.where(own, line, 0.0)
 
     def turn(i, carry):
-        @pl.when(i < strip)
-        def _():
-            pass_on(i)
-
-        @pl.when(relays & (i < strip) & (lax.rem(i, 2) == 1))
-        def _():
-            j = i // 2
-
-            @pl.when(lower)
-            def _():
-                to_relay(2 * j, 0).wait_recv()
-                from_relay(j, 0).start()
-
-            @pl.when(jnp.logical_not(lower))
-            def _():
-                to_relay(2 * j, 1).wait_recv()
-                from_relay(j, 1).start()
-
-        @pl.when(i >= AHEAD)
-        def _():
-            columns(i - AHEAD)
+        for side, here in ((0, lower), (1, jnp.logical_not(lower))):
+
+            @pl.when(here & ((near_relay & (lax.rem(i, 2) == 0)) | (far_relay & (lax.rem(i, 2) == 1))))
+            def _(side=side):
+                to_relay(i, side).wait_recv()
+                from_relay(i // 2, side).start()
+
+        pass_on(i, 0, next_left, next_right)
+        pass_on(i, 1, next_right, next_left)
+        for side, here in ((0, lower), (1, jnp.logical_not(lower))):
+
+            @pl.when(here & pass_relay & (i > 0))
+            def _(side=side):
+                pass_to_relay(i - 1, side).wait_recv()
+                pass_from_relay(i - 1, side).start()
 
         return carry
 
-    lax.fori_loop(0, strip + AHEAD, turn, 0)
+    lax.fori_loop(0, strip, turn, 0)
+    for side, here in ((0, lower), (1, jnp.logical_not(lower))):
+
+        @pl.when(here & pass_relay)
+        def _(side=side):
+            pass_to_relay(strip - 1, side).wait_recv()
+            pass_from_relay(strip - 1, side).start()
+
+    def last_turn(i, carry):
+        pass_on(i, 0, col == edge + 1, True)
+        pass_on(i, 1, col == edge, True)
+        columns(i)
+        return carry
+
+    lax.fori_loop(0, strip, last_turn, 0)
 
     def finish(i, carry):
         @pl.when(has_right)
@@ -356,6 +386,11 @@
     def _():
         for j in range(strip // 2):
             from_relay(j, 0).wait_send()
+
+    @pl.when(pass_relay)
+    def _():
+        for i in range(strip):
+            pass_from_relay(i, 0).wait_send()
 
 
     @pl.when(has_up)
@@ -392,6 +427,7 @@
                 pltpu.VMEM(block, BF16),
                 pltpu.VMEM(block, BF16),
                 pltpu.VMEM((strip // 2, nlon, cols_dev), BF16),
+                pltpu.VMEM((strip, nlon, nlon), BF16),
                 pltpu.VMEM((4, 256, 256), BF16),
                 pltpu.VMEM((4, 256, 256), BF16),
                 pltpu.SMEM((STEPS * (strip + 2 * STEPS) * 5,), F32),
@@ -405,8 +441,10 @@
                 pltpu.SemaphoreType.DMA((2, strip)),
                 pltpu.SemaphoreType.DMA((strip // 2,)),
                 pltpu.SemaphoreType.DMA((strip // 2,)),
+                pltpu.SemaphoreType.DMA((strip,)),
+                pltpu.SemaphoreType.DMA((strip,)),
             ],
-            compiler_params=pltpu.CompilerParams(collective_id=0, has_side_effects=True, vmem_limit_bytes=14 << 20),
+            compiler_params=pltpu.CompilerParams(collective_id=0, has_side_effects=True, vmem_limit_bytes=54755328),
         )(covariance.reshape(block), noise_var, wind_table.T, diffusivity, wind_index)
         return out.reshape(rows_dev, cols_dev), s.reshape(rows_dev, cols_dev)
 

time: 60.3 us -> 41.4 us (0.69)
  the two profiles are of different devices: /device:TPU:62 before, /device:TPU:54 now
where the time goes in v3:
time: 41.4 us; the launch traced here: 40.7 us
  Pallas kernels  36.9 us (89%)
  local copies, waits for them, and re-layouts  3.13 us (8%)
  between operations  0.67 us (2%)
    pallas_call x1, Pallas kernels, body(): pl.pallas_call(functools.partial(kernel, nlat, nrow, ncol), out_shape=(ja...  36.9 us
    unnamed x10, local copies, waits for them, and re-layouts  3.13 us

profile of v3, /device:TPU:54, one launch (start us, length us, event | category | flops | bytes accessed | tf_op | source)
XLA Modules:
  0.0 40.7 jit_solution(1180303143862418855)
XLA Ops:
  0.6 0.0 copy-start.1
  0.6 0.0 copy-start.2
  0.7 0.0 copy-start.3
  0.7 0.7 %copy-done.1 = s32[3,64]{1,0:T(4,128)S(1)} copy-done((s32[3,64]{1,0:T(4,128)S(1)}, s32[3,64]{1,0:T(4,128)}, u32[]{:S(2)}) %copy-start.1) | copy-done | bytes 792
  1.3 0.0 copy-done.2
  1.3 0.0 copy-done.3
  1.3 0.0 copy-start
  1.3 0.7 %copy-done = f32[8,128]{1,0:T(8,128)S(1)} copy-done((f32[8,128]{1,0:T(8,128)S(1)}, f32[8,128]{1,0:T(8,128)}, u32[]{:S(2)}) %copy-start) | copy-done | bytes 4120
  2.0 36.9 %shard_map.68 = (f32[8,128,256]{2,1,0:T(8,128)S(1)}, bf16[8,128,256]{2,1,0:T(8,128)(2,1)S(1)}) custom-call(f32[8,128,256]{2,1,0:T(8,128)} %bitcast.7, f32[8,128]{1,0:T(8,128)S(1)} %copy-done, f32[2,16]{1,0:T(2,128)S(1)} %bitcast.6, f32[16]{0:T(128)S(1)} %copy-done.3, s32[3,64]{1,0:T(4,128)S(1)} %copy-done.1), custom_call_target="tpu_custom_call" | custom-call | tf_op jit(solution)/shard_map/pallas_call | solution.py:416
  38.9 1.0 %copy.9 = f32[1024,256]{1,0:T(8,128)} copy(f32[1024,256]{1,0:T(8,128)S(1)} %bitcast.4) | data formatting | bytes 2097152
  39.9 0.8 %copy.10 = bf16[1024,256]{1,0:T(8,128)(2,1)} copy(bf16[1024,256]{1,0:T(8,128)(2,1)S(1)} %bitcast.5) | data formatting | bytes 1048576
Async XLA Ops:
  0.6 0.7 %copy-start.1 = (s32[3,64]{1,0:T(4,128)S(1)}, s32[3,64]{1,0:T(4,128)}, u32[]{:S(2)}) copy-start(s32[3,64]{1,0:T(4,128)} %index.1) | copy-start | bytes 2308
  0.6 0.7 %copy-start.2 = (f32[16,2]{0,1:T(2,128)S(1)}, f32[16,2]{0,1:T(2,128)}, u32[]{:S(2)}) copy-start(f32[16,2]{0,1:T(2,128)} %param.7) | copy-start | bytes 388
  0.7 0.7 %copy-start.3 = (f32[16]{0:T(128)S(1)}, f32[16]{0:T(128)}, u32[]{:S(2)}) copy-start(f32[16]{0:T(128)} %diffusivity.1) | copy-start | bytes 196
  1.3 0.7 %copy-start = (f32[8,128]{1,0:T(8,128)S(1)}, f32[8,128]{1,0:T(8,128)}, u32[]{:S(2)}) copy-start(f32[8,128]{1,0:T(8,128)} %noise.1) | copy-start | bytes 12292

commit v4 on v3

--- a/solution.py
+++ b/solution.py
@@ -18,31 +18,29 @@
     return jnp.where(i < 2, i + 3, jnp.where(even, jnp.where(i < 5, i + 3, i - 5), jnp.where(i < 5, i - 2, i)))
 
 
-def put_weights(dst, span, first_lat, nlat, table, diffusivity, index):
-    for step in range(STEPS):
-
-        def one(place, carry, step=step):
-            lat = first_lat + place
-            inside = jnp.where((lat >= 0) & (lat < nlat), 1.0, 0.0).astype(F32)
-            regime = index[step, jnp.clip(lat, 0, nlat - 1)]
-            zonal, merid, diffuse = table[0, regime], table[1, regime], diffusivity[regime]
-            zz, mm = 0.5 * zonal * zonal, 0.5 * merid * merid
-            at = (step * span + place) * 5
-            dst[at] = inside * (1.0 - zonal * zonal - merid * merid - 4.0 * diffuse)
-            dst[at + 1] = inside * (zz - 0.5 * zonal + diffuse)
-            dst[at + 2] = inside * (zz + 0.5 * zonal + diffuse)
-            dst[at + 3] = inside * (mm - 0.5 * merid + diffuse)
-            dst[at + 4] = inside * (mm + 0.5 * merid + diffuse)
-            return carry
-
-        lax.fori_loop(step + 1, span - 1 - step, one, 0)
+def put_weights(dst, table, diffusivity):
+    for regime in range(diffusivity.shape[0]):
+        zonal, merid, diffuse = table[0, regime], table[1, regime], diffusivity[regime]
+        zz, mm = 0.5 * zonal * zonal, 0.5 * merid * merid
+        dst[regime * 5] = 1.0 - zonal * zonal - merid * merid - 4.0 * diffuse
+        dst[regime * 5 + 1] = zz - 0.5 * zonal + diffuse
+        dst[regime * 5 + 2] = zz + 0.5 * zonal + diffuse
+        dst[regime * 5 + 3] = mm - 0.5 * merid + diffuse
+        dst[regime * 5 + 4] = mm + 0.5 * merid + diffuse
+
+
+def weights_at(weights, index, step, lat):
+    nlat = index.shape[1]
+    inside = jnp.where((lat >= 0) & (lat < nlat), 1.0, 0.0).astype(F32)
+    at = index[step, jnp.clip(lat, 0, nlat - 1)] * 5
+    return [inside * weights[at + n] for n in range(5)]
 
 
 def kernel(
     nlat, nrow, ncol,
     cov, noise, table, diffusivity, index,
     ob, sb,
-    buf0, buf1, buf2, low, l2, r2, far, held, held_far, w_high, w_low, w_row, w_col,
+    buf0, buf1, buf2, low, l2, r2, far, held, held_far, w_high, w_low, weights,
     load_sem, row_send, row_recv, one_send, one_recv, two_send, two_recv, held_send, held_recv, far_send, far_recv,
 ):
     strip, nlon, width = cov.shape
@@ -52,7 +50,6 @@
     next_left, next_right = has_left & (col != ncol // 2), has_right & (col != ncol // 2 - 1)
     up, down = (lax.rem(row + nrow - 1, nrow), col), (lax.rem(row + 1, nrow), col)
     left, right = (row, lax.rem(col + ncol - 1, ncol)), (row, lax.rem(col + 1, ncol))
-    span = strip + 2 * STEPS
 
     edge = ncol // 2 - 1
     near_relay = (col == 3) | (col == ncol - 4)
@@ -91,58 +88,6 @@
 
         count = count + jnp.where(there, 1, 0)
 
-    put_weights(w_row, span, row * strip - STEPS, nlat, table, diffusivity, index)
-    put_weights(w_col, 8, col * 2 - STEPS, nlat, table, diffusivity, index)
-
-    @pl.when(jnp.logical_not(has_up))
-    def _():
-        buf0[pl.ds(0, STEPS)] = jnp.zeros((STEPS, nlon, width), F32)
-
-    @pl.when(jnp.logical_not(has_down))
-    def _():
-        buf0[pl.ds(strip + STEPS, STEPS)] = jnp.zeros((STEPS, nlon, width), F32)
-
-    @pl.when(jnp.logical_not(has_left))
-    def _():
-        l2[...] = jnp.zeros(l2.shape, BF16)
-
-    @pl.when(jnp.logical_not(has_right))
-    def _():
-        r2[...] = jnp.zeros(r2.shape, BF16)
-
-    @pl.when(col <= 1)
-    def _():
-        far[:, :, 0:128] = jnp.zeros((strip, nlon, 128), BF16)
-
-    @pl.when(col >= ncol - 2)
-    def _():
-        far[:, :, 128:256] = jnp.zeros((strip, nlon, 128), BF16)
-
-    sub = lax.broadcasted_iota(jnp.int32, (8, 128), 0)
-    middle = lax.broadcasted_iota(jnp.int32, (8, 128), 1) == 64
-    v = [jnp.where((sub == n) & middle, 1.0, 0.0).astype(F32) for n in range(8)]
-    for step in range(STEPS):
-        fresh = []
-        for n in range(1, len(v) - 1):
-            at = (step * 8 + n + step) * 5
-            mid, east, west, north, south = (w_col[at + m] for m in range(5))
-            fresh.append(
-                mid * v[n]
-                + east * pltpu.roll(v[n], 127, 1)
-                + west * pltpu.roll(v[n], 1, 1)
-                + north * v[n + 1]
-                + south * v[n - 1]
-            )
-        v = fresh
-    for place, lat in enumerate((0, 7, 1, 2, 3, 4, 5, 6)):
-        for half in range(2):
-            line = jnp.broadcast_to(v[half][lat : lat + 1, :], (128, 128))
-            block = pltpu.roll(line, 64, 1, stride=1, stride_axis=0)
-            rows, lanes = pl.ds((place % 2) * 128, 128), pl.ds(half * 128, 128)
-            high = block.astype(BF16)
-            w_high[place // 2, rows, lanes] = high
-            w_low[place // 2, rows, lanes] = (block - high.astype(F32)).astype(BF16)
-
     pl.semaphore_wait(barrier, count)
 
     to_up = pltpu.make_async_remote_copy(
@@ -162,10 +107,11 @@
     def _():
         to_down.start()
 
+    first_row = row * strip - STEPS
+
     def rows_step(src, dst, step, first, last, base):
         def one(place, carry):
-            at = (step * span + place) * 5
-            mid, east, west, north, south = (w_row[at + n] for n in range(5))
+            mid, east, west, north, south = weights_at(weights, index, step, first_row + place)
             for half in range(width // 128):
                 lanes = pl.ds(half * 128, 128)
                 value = src[place, :, lanes]
@@ -242,6 +188,31 @@
 
         lax.fori_loop(start, stop, one, 0)
 
+    @pl.when(jnp.logical_not(has_up))
+    def _():
+        buf0[pl.ds(0, STEPS)] = jnp.zeros((STEPS, nlon, width), F32)
+
+    @pl.when(jnp.logical_not(has_down))
+    def _():
+        buf0[pl.ds(strip + STEPS, STEPS)] = jnp.zeros((STEPS, nlon, width), F32)
+
+    @pl.when(jnp.logical_not(has_left))
+    def _():
+        l2[...] = jnp.zeros(l2.shape, BF16)
+
+    @pl.when(jnp.logical_not(has_right))
+    def _():
+        r2[...] = jnp.zeros(r2.shape, BF16)
+
+    @pl.when(col <= 1)
+    def _():
+        far[:, :, 0:128] = jnp.zeros((strip, nlon, 128), BF16)
+
+    @pl.when(col >= ncol - 2)
+    def _():
+        far[:, :, 128:256] = jnp.zeros((strip, nlon, 128), BF16)
+
+    put_weights(weights, table, diffusivity)
     load.wait()
     rows_step(buf0, buf1, 0, 4, 10, 0)
     rows_step(buf1, buf2, 1, 5, 9, 0)
@@ -264,12 +235,6 @@
         ):
             first = jnp.where(bottom, bottom_first, top_first)
             rows_step(src, dst, step, first, first + STEPS, base)
-
-    even = lax.rem(row, 2) == 0
-    end_rows(even)
-    send_first(2, 5)
-    end_rows(jnp.logical_not(even))
-    send_first(5, 8)
 
     def pass_to_relay(i, side):
         lanes = (pl.ds(128, 128), pl.ds(0, 128))[side]
@@ -329,7 +294,7 @@
                 line = noise[pl.ds(lat, 1), :]
                 ob[lat, :, lanes] = ob[lat, :, lanes] + jnp.where(own, line, 0.0)
 
-    def turn(i, carry):
+    def relay_turn(i):
         for side, here in ((0, lower), (1, jnp.logical_not(lower))):
 
             @pl.when(here & ((near_relay & (lax.rem(i, 2) == 0)) | (far_relay & (lax.rem(i, 2) == 1))))
@@ -337,6 +302,47 @@
                 to_relay(i, side).wait_recv()
                 from_relay(i // 2, side).start()
 
+    def relay_turns(start, stop):
+        def one(i, carry):
+            relay_turn(i)
+            return carry
+
+        lax.fori_loop(start, stop, one, 0)
+
+    even = lax.rem(row, 2) == 0
+    relay_turns(0, 2)
+    end_rows(even)
+    send_first(2, 5)
+    relay_turns(2, 5)
+    sub = lax.broadcasted_iota(jnp.int32, (8, 128), 0)
+    middle = lax.broadcasted_iota(jnp.int32, (8, 128), 1) == 64
+    v = [jnp.where((sub == n) & middle, 1.0, 0.0).astype(F32) for n in range(8)]
+    for step in range(STEPS):
+        fresh = []
+        for n in range(1, len(v) - 1):
+            mid, east, west, north, south = weights_at(weights, index, step, 2 * col - STEPS + n + step)
+            fresh.append(
+                mid * v[n]
+                + east * pltpu.roll(v[n], 127, 1)
+                + west * pltpu.roll(v[n], 1, 1)
+                + north * v[n + 1]
+                + south * v[n - 1]
+            )
+        v = fresh
+    for place, lat in enumerate((0, 7, 1, 2, 3, 4, 5, 6)):
+        for half in range(2):
+            line = jnp.broadcast_to(v[half][lat : lat + 1, :], (128, 128))
+            block = pltpu.roll(line, 64, 1, stride=1, stride_axis=0)
+            rows, lanes = pl.ds((place % 2) * 128, 128), pl.ds(half * 128, 128)
+            high = block.astype(BF16)
+            w_high[place // 2, rows, lanes] = high
+            w_low[place // 2, rows, lanes] = (block - high.astype(F32)).astype(BF16)
+
+    def turn(i, carry):
+        @pl.when((i > 1) & (i < 5))
+        def _():
+            relay_turn(i + 3)
+
         pass_on(i, 0, next_left, next_right)
         pass_on(i, 1, next_right, next_left)
         for side, here in ((0, lower), (1, jnp.logical_not(lower))):
@@ -348,7 +354,10 @@
 
         return carry
 
-    lax.fori_loop(0, strip, turn, 0)
+    lax.fori_loop(0, 2, turn, 0)
+    end_rows(jnp.logical_not(even))
+    send_first(5, 8)
+    lax.fori_loop(2, strip, turn, 0)
     for side, here in ((0, lower), (1, jnp.logical_not(lower))):
 
         @pl.when(here & pass_relay)
@@ -430,8 +439,7 @@
                 pltpu.VMEM((strip, nlon, nlon), BF16),
                 pltpu.VMEM((4, 256, 256), BF16),
                 pltpu.VMEM((4, 256, 256), BF16),
-                pltpu.SMEM((STEPS * (strip + 2 * STEPS) * 5,), F32),
-                pltpu.SMEM((STEPS * 8 * 5,), F32),
+                pltpu.SMEM((5 * diffusivity.shape[0],), F32),
                 pltpu.SemaphoreType.DMA,
                 pltpu.SemaphoreType.DMA((2,)),
                 pltpu.SemaphoreType.DMA((2,)),

time: 41.4 us -> 37.9 us (0.915); the launches traced: 40.7 us -> 37.6 us
  Pallas kernels: 36.9 us -> 33.8 us
    pallas_call x1, Pallas kernels: 36.9 us -> 33.8 us  [body(): pl.pallas_call(functools.partial(kernel, nlat, nrow, ncol), out_shape=(ja...]
where the time goes in v4:
time: 37.9 us; the launch traced here: 37.6 us
  Pallas kernels  33.8 us (89%)
  local copies, waits for them, and re-layouts  3.13 us (8%)
  between operations  0.67 us (2%)
    pallas_call x1, Pallas kernels, body(): pl.pallas_call(functools.partial(kernel, nlat, nrow, ncol), out_shape=(ja...  33.8 us
    unnamed x10, local copies, waits for them, and re-layouts  3.13 us

profile of v4, /device:TPU:54, one launch (start us, length us, event | category | flops | bytes accessed | tf_op | source)
XLA Modules:
  0.0 37.6 jit_solution(4646260089356616800)
XLA Ops:
  0.6 0.0 copy-start.1
  0.6 0.0 copy-start.2
  0.7 0.0 copy-start.3
  0.7 0.7 %copy-done.1 = s32[3,64]{1,0:T(4,128)S(1)} copy-done((s32[3,64]{1,0:T(4,128)S(1)}, s32[3,64]{1,0:T(4,128)}, u32[]{:S(2)}) %copy-start.1) | copy-done | bytes 792
  1.3 0.0 copy-done.2
  1.3 0.0 copy-done.3
  1.3 0.0 copy-start
  1.3 0.7 %copy-done = f32[8,128]{1,0:T(8,128)S(1)} copy-done((f32[8,128]{1,0:T(8,128)S(1)}, f32[8,128]{1,0:T(8,128)}, u32[]{:S(2)}) %copy-start) | copy-done | bytes 4120
  2.0 33.8 %shard_map.68 = (f32[8,128,256]{2,1,0:T(8,128)S(1)}, bf16[8,128,256]{2,1,0:T(8,128)(2,1)S(1)}) custom-call(f32[8,128,256]{2,1,0:T(8,128)} %bitcast.7, f32[8,128]{1,0:T(8,128)S(1)} %copy-done, f32[2,16]{1,0:T(2,128)S(1)} %bitcast.6, f32[16]{0:T(128)S(1)} %copy-done.3, s32[3,64]{1,0:T(4,128)S(1)} %copy-done.1), custom_call_target="tpu_custom_call" | custom-call | tf_op jit(solution)/shard_map/pallas_call | solution.py:425
  35.8 1.0 %copy.9 = f32[1024,256]{1,0:T(8,128)} copy(f32[1024,256]{1,0:T(8,128)S(1)} %bitcast.4) | data formatting | bytes 2097152
  36.8 0.8 %copy.10 = bf16[1024,256]{1,0:T(8,128)(2,1)} copy(bf16[1024,256]{1,0:T(8,128)(2,1)S(1)} %bitcast.5) | data formatting | bytes 1048576
Async XLA Ops:
  0.6 0.7 %copy-start.1 = (s32[3,64]{1,0:T(4,128)S(1)}, s32[3,64]{1,0:T(4,128)}, u32[]{:S(2)}) copy-start(s32[3,64]{1,0:T(4,128)} %index.1) | copy-start | bytes 2308
  0.6 0.7 %copy-start.2 = (f32[16,2]{0,1:T(2,128)S(1)}, f32[16,2]{0,1:T(2,128)}, u32[]{:S(2)}) copy-start(f32[16,2]{0,1:T(2,128)} %param.7) | copy-start | bytes 388
  0.7 0.7 %copy-start.3 = (f32[16]{0:T(128)S(1)}, f32[16]{0:T(128)}, u32[]{:S(2)}) copy-start(f32[16]{0:T(128)} %diffusivity.1) | copy-start | bytes 196
  1.3 0.7 %copy-start = (f32[8,128]{1,0:T(8,128)S(1)}, f32[8,128]{1,0:T(8,128)}, u32[]{:S(2)}) copy-start(f32[8,128]{1,0:T(8,128)} %noise.1) | copy-start | bytes 12292

commit v5 on v4

--- a/solution.py
+++ b/solution.py
@@ -38,17 +38,20 @@
 
 def kernel(
     nlat, nrow, ncol,
-    cov, noise, table, diffusivity, index,
+    cov, noise_in, table_in, diffusivity_in, index_in,
     ob, sb,
-    buf0, buf1, buf2, low, l2, r2, far, held, held_far, w_high, w_low, weights,
-    load_sem, row_send, row_recv, one_send, one_recv, two_send, two_recv, held_send, held_recv, far_send, far_recv,
+    buf0, buf1, buf2, low, l2, r2, far, held, held_far, edge_out, edge_in, w_high, w_low, noise, table, diffusivity, index, weights,
+    ready, load_sem, small_sem, row_send, row_recv, one_send, one_recv, rest_send, rest_recv, two_send, two_recv, held_send, held_recv, far_send, far_recv,
 ):
     strip, nlon, width = cov.shape
     row, col = lax.axis_index("row"), lax.axis_index("col")
     has_up, has_down = row > 0, row < nrow - 1
     has_left, has_right = col > 0, col < ncol - 1
     next_left, next_right = has_left & (col != ncol // 2), has_right & (col != ncol // 2 - 1)
-    up, down = (lax.rem(row + nrow - 1, nrow), col), (lax.rem(row + 1, nrow), col)
+    even = lax.rem(row, 2) == 0
+    has_next = jnp.where(even, row, nrow - 1 - row) > 0
+    near_row = (jnp.where(even, row + 1, row - 1), col)
+    next_row = (lax.rem(jnp.where(even, row + nrow - 1, row + 1), nrow), col)
     left, right = (row, lax.rem(col + ncol - 1, ncol)), (row, lax.rem(col + 1, ncol))
 
     edge = ncol // 2 - 1
@@ -63,6 +66,14 @@
 
     load = pltpu.make_async_copy(cov, buf0.at[pl.ds(STEPS, strip)], load_sem)
     load.start()
+    small = [
+        pltpu.make_async_copy(src, dst, small_sem.at[n])
+        for n, (src, dst) in enumerate(
+            ((index_in, index), (table_in, table), (diffusivity_in, diffusivity), (noise_in, noise))
+        )
+    ]
+    for copy in small:
+        copy.start()
 
     barrier = pltpu.get_barrier_semaphore()
 
@@ -72,15 +83,16 @@
             jnp.where(lower, ncol - 4, 0),
             jnp.where(lower, ncol - 1, 3),
             jnp.where(lower, ncol - 8, 7),
+            jnp.where(lower, 0, ncol - 1),
         ):
             pl.semaphore_signal(barrier, inc=1, device_id=(row, peer), device_id_type=MESH)
 
-    @pl.when(relays | pass_relay)
+    @pl.when(near_relay | pass_relay)
     def _():
         pl.semaphore_signal(barrier, inc=1, device_id=(row, relay_from), device_id_type=MESH)
 
-    count = jnp.where(at_edge, 3, 0) + jnp.where(relays | pass_relay, 1, 0)
-    for there, peer in ((has_up, up), (has_down, down), (next_left, left), (next_right, right)):
+    count = jnp.where(at_edge | far_relay, 2, 0) + jnp.where(near_relay | pass_relay, 1, 0)
+    for there, peer in ((has_next, next_row), (row >= 0, near_row), (next_left, left), (next_right, right)):
 
         @pl.when(there)
         def _(peer=peer):
@@ -88,24 +100,29 @@
 
         count = count + jnp.where(there, 1, 0)
 
+    load.wait()
+    edge_out[...] = buf0[pl.ds(jnp.where(even, STEPS, strip), STEPS)].astype(BF16)
     pl.semaphore_wait(barrier, count)
 
-    to_up = pltpu.make_async_remote_copy(
-        src_ref=cov.at[pl.ds(0, STEPS)], dst_ref=buf0.at[pl.ds(strip + STEPS, STEPS)],
-        send_sem=row_send.at[0], recv_sem=row_recv.at[0], device_id=up, device_id_type=MESH,
+    @pl.when(far_relay)
+    def _():
+        pl.semaphore_signal(ready, inc=1, device_id=(row, relay_from), device_id_type=MESH)
+
+    to_near = pltpu.make_async_remote_copy(
+        src_ref=cov.at[pl.ds(jnp.where(even, strip - STEPS, 0), STEPS)],
+        dst_ref=buf0.at[pl.ds(jnp.where(even, 0, strip + STEPS), STEPS)],
+        send_sem=row_send.at[0], recv_sem=row_recv.at[0], device_id=near_row, device_id_type=MESH,
     )
-    to_down = pltpu.make_async_remote_copy(
-        src_ref=cov.at[pl.ds(strip - STEPS, STEPS)], dst_ref=buf0.at[pl.ds(0, STEPS)],
-        send_sem=row_send.at[1], recv_sem=row_recv.at[1], device_id=down, device_id_type=MESH,
+    to_next = pltpu.make_async_remote_copy(
+        src_ref=edge_out, dst_ref=edge_in,
+        send_sem=row_send.at[1], recv_sem=row_recv.at[1], device_id=next_row, device_id_type=MESH,
     )
 
-    @pl.when(has_up)
-    def _():
-        to_up.start()
-
-    @pl.when(has_down)
-    def _():
-        to_down.start()
+    @pl.when(has_next)
+    def _():
+        to_next.start()
+
+    to_near.start()
 
     first_row = row * strip - STEPS
 
@@ -132,13 +149,18 @@
 
         lax.fori_loop(first, last, one, 0)
 
+    def piece(i, side, near):
+        lat = chunk_of(i)
+        lanes = pl.ds(128 if (side == 0) == near else 0, 128)
+        send, recv = (one_send, one_recv) if near else (rest_send, rest_recv)
+        return pltpu.make_async_remote_copy(
+            src_ref=sb.at[lat, :, lanes], dst_ref=(l2, r2)[side].at[lat, :, lanes],
+            send_sem=send.at[side, i], recv_sem=recv.at[side, i],
+            device_id=(right, left)[side], device_id_type=MESH,
+        )
+
     def first_message(i, side):
-        lat = chunk_of(i)
-        return pltpu.make_async_remote_copy(
-            src_ref=sb.at[lat], dst_ref=(l2, r2)[side].at[lat],
-            send_sem=one_send.at[side, i], recv_sem=one_recv.at[side, i],
-            device_id=(right, left)[side], device_id_type=MESH,
-        )
+        return piece(i, side, True)
 
     def to_relay(i, side):
         near, away = ((3, 0), (ncol - 4, ncol - 1))[side]
@@ -148,8 +170,7 @@
             device_id=(row, jnp.where(lax.rem(i, 2) == 0, near, away)), device_id_type=MESH,
         )
 
-    def from_relay(j, side):
-        i = 2 * j + jnp.where(near_relay, 0, 1)
+    def from_relay(j, side, i):
         return pltpu.make_async_remote_copy(
             src_ref=held.at[j], dst_ref=(l2, r2)[side].at[chunk_of(i)],
             send_sem=held_send.at[j], recv_sem=one_recv.at[side, i],
@@ -166,26 +187,48 @@
             device_id=(right, left)[side], device_id_type=MESH,
         )
 
-    def send_first(start, stop):
+    def send_near(start, stop):
         def one(i, carry):
-            @pl.when(has_right & (col != edge))
+            @pl.when(next_right)
             def _():
                 first_message(i, 0).start()
 
+            @pl.when(next_left)
+            def _():
+                first_message(i, 1).start()
+
+            return carry
+
+        lax.fori_loop(start, stop, one, 0)
+
+    def send_far(start, stop, by):
+        def one(n, carry):
+            i = start + n * by
+
             @pl.when(col == edge)
             def _():
                 to_relay(i, 0).start()
 
-            @pl.when(has_left & (col != edge + 1))
-            def _():
-                first_message(i, 1).start()
-
             @pl.when(col == edge + 1)
             def _():
                 to_relay(i, 1).start()
 
             return carry
 
+        lax.fori_loop(0, (stop - start + by - 1) // by, one, 0)
+
+    def send_rest(start, stop):
+        def one(i, carry):
+            @pl.when(next_right)
+            def _():
+                piece(i, 0, False).start()
+
+            @pl.when(next_left)
+            def _():
+                piece(i, 1, False).start()
+
+            return carry
+
         lax.fori_loop(start, stop, one, 0)
 
     @pl.when(jnp.logical_not(has_up))
@@ -212,22 +255,17 @@
     def _():
         far[:, :, 128:256] = jnp.zeros((strip, nlon, 128), BF16)
 
+    for copy in small:
+        copy.wait()
     put_weights(weights, table, diffusivity)
-    load.wait()
     rows_step(buf0, buf1, 0, 4, 10, 0)
     rows_step(buf1, buf2, 1, 5, 9, 0)
     rows_step(buf2, low, 2, 6, 8, STEPS)
-    send_first(0, 2)
+    send_near(0, 2)
+    send_far(0, 1, 1)
+    send_rest(0, 2)
 
     def end_rows(bottom):
-        @pl.when(jnp.logical_not(bottom) & has_up)
-        def _():
-            to_down.wait_recv()
-
-        @pl.when(bottom & has_down)
-        def _():
-            to_up.wait_recv()
-
         for src, dst, step, top_first, bottom_first, base in (
             (buf0, buf1, 0, 1, strip + 2, 0),
             (buf1, buf2, 1, 2, strip + 1, 0),
@@ -266,6 +304,14 @@
 
     def columns(i):
         lat = chunk_of(i)
+
+        @pl.when(next_left)
+        def _():
+            piece(i, 0, False).wait_recv()
+
+        @pl.when(next_right)
+        def _():
+            piece(i, 1, False).wait_recv()
 
         @pl.when(col > 1)
         def _():
@@ -300,7 +346,7 @@
             @pl.when(here & ((near_relay & (lax.rem(i, 2) == 0)) | (far_relay & (lax.rem(i, 2) == 1))))
             def _(side=side):
                 to_relay(i, side).wait_recv()
-                from_relay(i // 2, side).start()
+                from_relay(i // 2, side, i).start()
 
     def relay_turns(start, stop):
         def one(i, carry):
@@ -309,11 +355,18 @@
 
         lax.fori_loop(start, stop, one, 0)
 
-    even = lax.rem(row, 2) == 0
-    relay_turns(0, 2)
+    relay_turns(0, 1)
+    to_near.wait_recv()
     end_rows(even)
-    send_first(2, 5)
-    relay_turns(2, 5)
+    send_near(2, 5)
+    send_rest(2, 4)
+
+    @pl.when(at_edge)
+    def _():
+        pl.semaphore_wait(ready, 1)
+
+    send_far(1, 5, 1)
+    relay_turns(1, 3)
     sub = lax.broadcasted_iota(jnp.int32, (8, 128), 0)
     middle = lax.broadcasted_iota(jnp.int32, (8, 128), 1) == 64
     v = [jnp.where((sub == n) & middle, 1.0, 0.0).astype(F32) for n in range(8)]
@@ -343,44 +396,85 @@
         def _():
             relay_turn(i + 3)
 
+        @pl.when(pass_relay & jnp.logical_not(lower))
+        def _():
+            def one(n, carry):
+                pass_to_relay(n, 1).wait_recv()
+                pass_from_relay(n, 1).start()
+                return carry
+
+            lax.fori_loop(i + jnp.where(i > 2, 1, 0), jnp.minimum(i + jnp.where(i > 1, 2, 1), strip), one, 0)
+
         pass_on(i, 0, next_left, next_right)
         pass_on(i, 1, next_right, next_left)
-        for side, here in ((0, lower), (1, jnp.logical_not(lower))):
-
-            @pl.when(here & pass_relay & (i > 0))
-            def _(side=side):
-                pass_to_relay(i - 1, side).wait_recv()
-                pass_from_relay(i - 1, side).start()
+        @pl.when(pass_relay & lower & (i > 0))
+        def _():
+            pass_to_relay(i - 1, 0).wait_recv()
+            pass_from_relay(i - 1, 0).start()
 
         return carry
 
     lax.fori_loop(0, 2, turn, 0)
+
+    @pl.when(has_next)
+    def _():
+        to_next.wait_recv()
+        buf0[pl.ds(jnp.where(even, 0, strip + STEPS), STEPS)] = edge_in[...].astype(F32)
+
     end_rows(jnp.logical_not(even))
-    send_first(5, 8)
+    send_near(5, 8)
+    send_far(5, 8, 1)
+    send_rest(4, 8)
+    relay_turns(3, 5)
     lax.fori_loop(2, strip, turn, 0)
-    for side, here in ((0, lower), (1, jnp.logical_not(lower))):
-
-        @pl.when(here & pass_relay)
-        def _(side=side):
-            pass_to_relay(strip - 1, side).wait_recv()
-            pass_from_relay(strip - 1, side).start()
+    @pl.when(pass_relay & lower)
+    def _():
+        pass_to_relay(strip - 1, 0).wait_recv()
+        pass_from_relay(strip - 1, 0).start()
+
+    def edge_turn(i, carry):
+        @pl.when(col == edge + 1)
+        def _():
+            from_relay(i // 2, 0, i).wait_recv()
+            second_message(i, 0).start()
+
+        @pl.when(col == edge)
+        def _():
+            from_relay(i // 2, 1, i).wait_recv()
+            second_message(i, 1).start()
+
+        return carry
+
+    @pl.when(at_edge)
+    def _():
+        lax.fori_loop(0, strip, edge_turn, 0)
 
     def last_turn(i, carry):
-        pass_on(i, 0, col == edge + 1, True)
-        pass_on(i, 1, col == edge, True)
         columns(i)
         return carry
 
     lax.fori_loop(0, strip, last_turn, 0)
 
     def finish(i, carry):
-        @pl.when(has_right)
+        @pl.when(next_right)
         def _():
             first_message(i, 0).wait_send()
-
-        @pl.when(has_left)
+            piece(i, 0, False).wait_send()
+
+        @pl.when(next_left)
         def _():
             first_message(i, 1).wait_send()
+            piece(i, 1, False).wait_send()
+
+        @pl.when(at_edge)
+        def _():
+            @pl.when(lower)
+            def _():
+                to_relay(i, 0).wait_send()
+
+            @pl.when(jnp.logical_not(lower))
+            def _():
+                to_relay(i, 1).wait_send()
 
         @pl.when(has_left & has_right)
         def _():
@@ -394,7 +488,7 @@
     @pl.when(relays)
     def _():
         for j in range(strip // 2):
-            from_relay(j, 0).wait_send()
+            from_relay(j, 0, 2 * j).wait_send()
 
     @pl.when(pass_relay)
     def _():
@@ -402,13 +496,22 @@
             pass_from_relay(i, 0).wait_send()
 
 
-    @pl.when(has_up)
-    def _():
-        to_up.wait_send()
-
-    @pl.when(has_down)
-    def _():
-        to_down.wait_send()
+    to_near.wait_send()
+
+    @pl.when(has_next)
+    def _():
+        to_next.wait_send()
+
+
+def write_out(out_in, s_in, out, s, sem):
+    copies = []
+    for lat in range(out.shape[0]):
+        copies.append(pltpu.make_async_copy(out_in.at[lat], out.at[lat], sem.at[0, lat]))
+        copies.append(pltpu.make_async_copy(s_in.at[lat], s.at[lat], sem.at[1, lat]))
+    for copy in copies:
+        copy.start()
+    for copy in copies:
+        copy.wait()
 
 
 def solution(mesh):
@@ -421,11 +524,10 @@
         block = (strip, nlon, cols_dev)
         span = (strip + 2 * STEPS, nlon, cols_dev)
         anywhere = pl.BlockSpec(memory_space=pltpu.HBM)
-        scalars = pl.BlockSpec(memory_space=pltpu.SMEM)
-        out, s = pl.pallas_call(
+        held_out, held_s = pl.pallas_call(
             functools.partial(kernel, nlat, nrow, ncol),
             out_shape=(jax.ShapeDtypeStruct(block, F32), jax.ShapeDtypeStruct(block, BF16)),
-            in_specs=[anywhere, pl.BlockSpec(memory_space=pltpu.VMEM), scalars, scalars, scalars],
+            in_specs=[anywhere] * 5,
             out_specs=(pl.BlockSpec(memory_space=pltpu.VMEM),) * 2,
             scratch_shapes=[
                 pltpu.VMEM(span, F32),
@@ -437,12 +539,22 @@
                 pltpu.VMEM(block, BF16),
                 pltpu.VMEM((strip // 2, nlon, cols_dev), BF16),
                 pltpu.VMEM((strip, nlon, nlon), BF16),
+                pltpu.VMEM((STEPS, nlon, cols_dev), BF16),
+                pltpu.VMEM((STEPS, nlon, cols_dev), BF16),
                 pltpu.VMEM((4, 256, 256), BF16),
                 pltpu.VMEM((4, 256, 256), BF16),
+                pltpu.VMEM(noise_var.shape, F32),
+                pltpu.SMEM(wind_table.shape[::-1], F32),
+                pltpu.SMEM(diffusivity.shape, F32),
+                pltpu.SMEM(wind_index.shape, jnp.int32),
                 pltpu.SMEM((5 * diffusivity.shape[0],), F32),
+                pltpu.SemaphoreType.REGULAR,
                 pltpu.SemaphoreType.DMA,
+                pltpu.SemaphoreType.DMA((4,)),
                 pltpu.SemaphoreType.DMA((2,)),
                 pltpu.SemaphoreType.DMA((2,)),
+                pltpu.SemaphoreType.DMA((2, strip)),
+                pltpu.SemaphoreType.DMA((2, strip)),
                 pltpu.SemaphoreType.DMA((2, strip)),
                 pltpu.SemaphoreType.DMA((2, strip)),
                 pltpu.SemaphoreType.DMA((2, strip)),
@@ -453,7 +565,18 @@
                 pltpu.SemaphoreType.DMA((strip,)),
             ],
             compiler_params=pltpu.CompilerParams(collective_id=0, has_side_effects=True, vmem_limit_bytes=54755328),
-        )(covariance.reshape(block), noise_var, wind_table.T, diffusivity, wind_index)
+        )(*(
+            pltpu.with_memory_space_constraint(x, pltpu.HBM)
+            for x in (covariance.reshape(block), noise_var, wind_table.T, diffusivity, wind_index)
+        ))
+        out, s = pl.pallas_call(
+            write_out,
+            out_shape=(jax.ShapeDtypeStruct(block, F32), jax.ShapeDtypeStruct(block, BF16)),
+            in_specs=[pl.BlockSpec(memory_space=pltpu.VMEM)] * 2,
+            out_specs=(anywhere, anywhere),
+            scratch_shapes=[pltpu.SemaphoreType.DMA((2, strip))],
+            compiler_params=pltpu.CompilerParams(vmem_limit_bytes=1 << 20),
+        )(held_out, held_s)
         return out.reshape(rows_dev, cols_dev), s.reshape(rows_dev, cols_dev)
 
     in_specs = (P("row", "col"), P("row", None), P(), P(), P())

time: 37.9 us -> 34.1 us (0.90)
  local copies, waits for them, and re-layouts: 3.13 us -> 0 us
  Pallas kernels: 33.8 us -> 33.4 us
    unnamed x10 -> x0, local copies, waits for them, and re-layouts: 3.13 us -> none
    pallas_call x1, Pallas kernels: 33.8 us -> 32.1 us  [body(): pl.pallas_call(functools.partial(kernel, nlat, nrow, ncol), out_shape=(ja...]
    pallas_call x0 -> x1, Pallas kernels: none -> 1.26 us  [body(): pl.pallas_call(write_out, out_shape=(jax.ShapeDtypeStruct(block, F32), ja...]
where the time goes in v5:
time: 34.1 us; the launch traced here: 34 us
  Pallas kernels  33.4 us (98%)
  between operations  0.64 us (2%)
    pallas_call x1, Pallas kernels, body(): pl.pallas_call(functools.partial(kernel, nlat, nrow, ncol), out_shape=(ja...  32.1 us
    pallas_call x1, Pallas kernels, body(): pl.pallas_call(write_out, out_shape=(jax.ShapeDtypeStruct(block, F32), ja...  1.26 us

profile of v5, /device:TPU:54, one launch (start us, length us, event | category | flops | bytes accessed | tf_op | source)
XLA Modules:
  0.0 34.0 jit_solution(4907650315553963932)
XLA Ops:
  0.6 32.1 %shard_map.68 = (f32[8,128,256]{2,1,0:T(8,128)S(1)}, bf16[8,128,256]{2,1,0:T(8,128)(2,1)S(1)}) custom-call(f32[8,128,256]{2,1,0:T(8,128)} %bitcast.4, f32[8,128]{1,0:T(8,128)} %noise_in.1, f32[2,16]{1,0:T(2,128)} %bitcast.5, f32[16]{0:T(128)} %diffusivity_in.1, s32[3,64]{1,0:T(4,128)} %index_in.1), custom_call_target="tpu_custom_call" | custom-call | tf_op jit(solution)/shard_map/pallas_call | solution.py:527
  32.7 1.3 %shard_map.69 = (f32[8,128,256]{2,1,0:T(8,128)}, bf16[8,128,256]{2,1,0:T(8,128)(2,1)}) custom-call(f32[8,128,256]{2,1,0:T(8,128)S(1)} %get-tuple-element.6.out_in, bf16[8,128,256]{2,1,0:T(8,128)(2,1)S(1)} %get-tuple-element.7.s_in), custom_call_target="tpu_custom_call" | custom-call | tf_op jit(solution)/shard_map/pallas_call | solution.py:572

commit v6 on v5

--- a/solution.py
+++ b/solution.py
@@ -11,6 +11,7 @@
 F32 = jnp.float32
 BF16 = jnp.bfloat16
 STEPS = 3
+LAG = 3
 
 
 def chunk_of(i):
@@ -41,7 +42,7 @@
     cov, noise_in, table_in, diffusivity_in, index_in,
     ob, sb,
     buf0, buf1, buf2, low, l2, r2, far, held, held_far, edge_out, edge_in, w_high, w_low, noise, table, diffusivity, index, weights,
-    ready, load_sem, small_sem, row_send, row_recv, one_send, one_recv, rest_send, rest_recv, two_send, two_recv, held_send, held_recv, far_send, far_recv,
+    ready, load_sem, small_sem, row_send, row_recv, one_send, one_recv, rest_recv, two_send, held_send, held_recv, far_send, far_recv,
 ):
     strip, nlon, width = cov.shape
     row, col = lax.axis_index("row"), lax.axis_index("col")
@@ -152,10 +153,10 @@
     def piece(i, side, near):
         lat = chunk_of(i)
         lanes = pl.ds(128 if (side == 0) == near else 0, 128)
-        send, recv = (one_send, one_recv) if near else (rest_send, rest_recv)
+        recv = one_recv if near else rest_recv
         return pltpu.make_async_remote_copy(
             src_ref=sb.at[lat, :, lanes], dst_ref=(l2, r2)[side].at[lat, :, lanes],
-            send_sem=send.at[side, i], recv_sem=recv.at[side, i],
+            send_sem=one_send.at[side], recv_sem=recv.at[side, i],
             device_id=(right, left)[side], device_id_type=MESH,
         )
 
@@ -166,14 +167,14 @@
         near, away = ((3, 0), (ncol - 4, ncol - 1))[side]
         return pltpu.make_async_remote_copy(
             src_ref=sb.at[chunk_of(i)], dst_ref=held.at[i // 2],
-            send_sem=one_send.at[side, i], recv_sem=held_recv.at[i // 2],
+            send_sem=one_send.at[side], recv_sem=held_recv.at[i // 2],
             device_id=(row, jnp.where(lax.rem(i, 2) == 0, near, away)), device_id_type=MESH,
         )
 
     def from_relay(j, side, i):
         return pltpu.make_async_remote_copy(
             src_ref=held.at[j], dst_ref=(l2, r2)[side].at[chunk_of(i)],
-            send_sem=held_send.at[j], recv_sem=one_recv.at[side, i],
+            send_sem=held_send, recv_sem=one_recv.at[side, i],
             device_id=(row, relay_to), device_id_type=MESH,
         )
 
@@ -183,7 +184,7 @@
         return pltpu.make_async_remote_copy(
             src_ref=(l2, r2)[side].at[lat, :, lanes],
             dst_ref=far.at[lat, :, pl.ds(side * 128, 128)],
-            send_sem=two_send.at[side, i], recv_sem=two_recv.at[side, i],
+            send_sem=two_send.at[side], recv_sem=rest_recv.at[side, i],
             device_id=(right, left)[side], device_id_type=MESH,
         )
 
@@ -278,14 +279,14 @@
         lanes = (pl.ds(128, 128), pl.ds(0, 128))[side]
         return pltpu.make_async_remote_copy(
             src_ref=(l2, r2)[side].at[chunk_of(i), :, lanes], dst_ref=held_far.at[i],
-            send_sem=two_send.at[side, i], recv_sem=far_recv.at[i],
+            send_sem=two_send.at[side], recv_sem=far_recv.at[i],
             device_id=(row, (7, ncol - 8)[side]), device_id_type=MESH,
         )
 
     def pass_from_relay(i, side):
         return pltpu.make_async_remote_copy(
             src_ref=held_far.at[i], dst_ref=far.at[chunk_of(i), :, pl.ds(side * 128, 128)],
-            send_sem=far_send.at[i], recv_sem=two_recv.at[side, i],
+            send_sem=far_send, recv_sem=rest_recv.at[side, i],
             device_id=(row, relay_to), device_id_type=MESH,
         )
 
@@ -302,24 +303,34 @@
             def _():
                 pass_to_relay(i, side).start()
 
+    def arrival(like, recv):
+        return pltpu.make_async_remote_copy(
+            src_ref=like, dst_ref=like, send_sem=held_send, recv_sem=recv,
+            device_id=right, device_id_type=MESH,
+        )
+
+    def departure(like, send):
+        return pltpu.make_async_remote_copy(
+            src_ref=like, dst_ref=like, send_sem=send, recv_sem=far_recv.at[0],
+            device_id=right, device_id_type=MESH,
+        )
+
     def columns(i):
         lat = chunk_of(i)
 
-        @pl.when(next_left)
-        def _():
-            piece(i, 0, False).wait_recv()
-
-        @pl.when(next_right)
-        def _():
-            piece(i, 1, False).wait_recv()
-
-        @pl.when(col > 1)
-        def _():
-            second_message(i, 0).wait_recv()
-
-        @pl.when(col < ncol - 2)
-        def _():
-            second_message(i, 1).wait_recv()
+        for side, rest, passed in ((0, next_left, col > 1), (1, next_right, col < ncol - 2)):
+
+            @pl.when(rest & passed)
+            def _(side=side):
+                arrival(sb.at[lat], rest_recv.at[side, i]).wait_recv()
+
+            @pl.when(rest & jnp.logical_not(passed))
+            def _(side=side):
+                piece(i, side, False).wait_recv()
+
+            @pl.when(passed & jnp.logical_not(rest))
+            def _(side=side):
+                second_message(i, side).wait_recv()
 
         def dot(x, w):
             return jnp.dot(x, w, preferred_element_type=F32)
@@ -445,56 +456,36 @@
 
         return carry
 
-    @pl.when(at_edge)
-    def _():
-        lax.fori_loop(0, strip, edge_turn, 0)
-
     def last_turn(i, carry):
-        columns(i)
+        @pl.when(i < strip)
+        def _():
+            edge_turn(i, 0)
+
+        @pl.when(i >= LAG)
+        def _():
+            columns(i - LAG)
+
         return carry
 
-    lax.fori_loop(0, strip, last_turn, 0)
-
-    def finish(i, carry):
-        @pl.when(next_right)
-        def _():
-            first_message(i, 0).wait_send()
-            piece(i, 0, False).wait_send()
-
-        @pl.when(next_left)
-        def _():
-            first_message(i, 1).wait_send()
-            piece(i, 1, False).wait_send()
-
-        @pl.when(at_edge)
-        def _():
-            @pl.when(lower)
-            def _():
-                to_relay(i, 0).wait_send()
-
-            @pl.when(jnp.logical_not(lower))
-            def _():
-                to_relay(i, 1).wait_send()
+    lax.fori_loop(0, strip + LAG, last_turn, 0)
+
+    for side, there in ((0, has_right), (1, has_left)):
+
+        @pl.when(there)
+        def _(side=side):
+            departure(sb, one_send.at[side]).wait_send()
 
         @pl.when(has_left & has_right)
-        def _():
-            second_message(i, 0).wait_send()
-            second_message(i, 1).wait_send()
-
-        return carry
-
-    lax.fori_loop(0, strip, finish, 0)
+        def _(side=side):
+            departure(held_far, two_send.at[side]).wait_send()
 
     @pl.when(relays)
     def _():
-        for j in range(strip // 2):
-            from_relay(j, 0, 2 * j).wait_send()
+        departure(held, held_send).wait_send()
 
     @pl.when(pass_relay)
     def _():
-        for i in range(strip):
-            pass_from_relay(i, 0).wait_send()
-
+        departure(held_far, far_send).wait_send()
 
     to_near.wait_send()
 
@@ -553,15 +544,13 @@
                 pltpu.SemaphoreType.DMA((4,)),
                 pltpu.SemaphoreType.DMA((2,)),
                 pltpu.SemaphoreType.DMA((2,)),
+                pltpu.SemaphoreType.DMA((2,)),
                 pltpu.SemaphoreType.DMA((2, strip)),
                 pltpu.SemaphoreType.DMA((2, strip)),
-                pltpu.SemaphoreType.DMA((2, strip)),
-                pltpu.SemaphoreType.DMA((2, strip)),
-                pltpu.SemaphoreType.DMA((2, strip)),
-                pltpu.SemaphoreType.DMA((2, strip)),
+                pltpu.SemaphoreType.DMA((2,)),
+                pltpu.SemaphoreType.DMA,
                 pltpu.SemaphoreType.DMA((strip // 2,)),
-                pltpu.SemaphoreType.DMA((strip // 2,)),
-                pltpu.SemaphoreType.DMA((strip,)),
+                pltpu.SemaphoreType.DMA,
                 pltpu.SemaphoreType.DMA((strip,)),
             ],
             compiler_params=pltpu.CompilerParams(collective_id=0, has_side_effects=True, vmem_limit_bytes=54755328),

time: 34.1 us -> 33.3 us (0.977)
  Pallas kernels: 33.4 us -> 32.5 us
    pallas_call x1, Pallas kernels: 32.1 us -> 31.3 us  [body(): pl.pallas_call(functools.partial(kernel, nlat, nrow, ncol), out_shape=(ja...]
where the time goes in v6:
time: 33.3 us; the launch traced here: 33.2 us
  Pallas kernels  32.5 us (98%)
  between operations  0.64 us (2%)
    pallas_call x1, Pallas kernels, body(): pl.pallas_call(functools.partial(kernel, nlat, nrow, ncol), out_shape=(ja...  31.3 us
    pallas_call x1, Pallas kernels, body(): pl.pallas_call(write_out, out_shape=(jax.ShapeDtypeStruct(block, F32), ja...  1.26 us

profile of v6, /device:TPU:54, one launch (start us, length us, event | category | flops | bytes accessed | tf_op | source)
XLA Modules:
  0.0 33.2 jit_solution(5562562364402753629)
XLA Ops:
  0.6 31.3 %shard_map.68 = (f32[8,128,256]{2,1,0:T(8,128)S(1)}, bf16[8,128,256]{2,1,0:T(8,128)(2,1)S(1)}) custom-call(f32[8,128,256]{2,1,0:T(8,128)} %bitcast.4, f32[8,128]{1,0:T(8,128)} %noise_in.1, f32[2,16]{1,0:T(2,128)} %bitcast.5, f32[16]{0:T(128)} %diffusivity_in.1, s32[3,64]{1,0:T(4,128)} %index_in.1), custom_call_target="tpu_custom_call" | custom-call | tf_op jit(solution)/shard_map/pallas_call | solution.py:518
  31.9 1.3 %shard_map.69 = (f32[8,128,256]{2,1,0:T(8,128)}, bf16[8,128,256]{2,1,0:T(8,128)(2,1)}) custom-call(f32[8,128,256]{2,1,0:T(8,128)S(1)} %get-tuple-element.6.out_in, bf16[8,128,256]{2,1,0:T(8,128)(2,1)S(1)} %get-tuple-element.7.s_in), custom_call_target="tpu_custom_call" | custom-call | tf_op jit(solution)/shard_map/pallas_call | solution.py:561

commit v7 on v6

--- a/solution.py
+++ b/solution.py
@@ -12,6 +12,7 @@
 BF16 = jnp.bfloat16
 STEPS = 3
 LAG = 3
+JOINT = 5
 
 
 def chunk_of(i):
@@ -42,7 +43,7 @@
     cov, noise_in, table_in, diffusivity_in, index_in,
     ob, sb,
     buf0, buf1, buf2, low, l2, r2, far, held, held_far, edge_out, edge_in, w_high, w_low, noise, table, diffusivity, index, weights,
-    ready, load_sem, small_sem, row_send, row_recv, one_send, one_recv, rest_recv, two_send, held_send, held_recv, far_send, far_recv,
+    ready, load_sem, small_sem, row_send, row_recv, one_send, one_recv, rest_recv, two_send, two_recv, held_send, held_recv, far_send, far_recv,
 ):
     strip, nlon, width = cov.shape
     row, col = lax.axis_index("row"), lax.axis_index("col")
@@ -103,28 +104,6 @@
 
     load.wait()
     edge_out[...] = buf0[pl.ds(jnp.where(even, STEPS, strip), STEPS)].astype(BF16)
-    pl.semaphore_wait(barrier, count)
-
-    @pl.when(far_relay)
-    def _():
-        pl.semaphore_signal(ready, inc=1, device_id=(row, relay_from), device_id_type=MESH)
-
-    to_near = pltpu.make_async_remote_copy(
-        src_ref=cov.at[pl.ds(jnp.where(even, strip - STEPS, 0), STEPS)],
-        dst_ref=buf0.at[pl.ds(jnp.where(even, 0, strip + STEPS), STEPS)],
-        send_sem=row_send.at[0], recv_sem=row_recv.at[0], device_id=near_row, device_id_type=MESH,
-    )
-    to_next = pltpu.make_async_remote_copy(
-        src_ref=edge_out, dst_ref=edge_in,
-        send_sem=row_send.at[1], recv_sem=row_recv.at[1], device_id=next_row, device_id_type=MESH,
-    )
-
-    @pl.when(has_next)
-    def _():
-        to_next.start()
-
-    to_near.start()
-
     first_row = row * strip - STEPS
 
     def rows_step(src, dst, step, first, last, base):
@@ -150,111 +129,13 @@
 
         lax.fori_loop(first, last, one, 0)
 
-    def piece(i, side, near):
-        lat = chunk_of(i)
-        lanes = pl.ds(128 if (side == 0) == near else 0, 128)
-        recv = one_recv if near else rest_recv
-        return pltpu.make_async_remote_copy(
-            src_ref=sb.at[lat, :, lanes], dst_ref=(l2, r2)[side].at[lat, :, lanes],
-            send_sem=one_send.at[side], recv_sem=recv.at[side, i],
-            device_id=(right, left)[side], device_id_type=MESH,
-        )
-
-    def first_message(i, side):
-        return piece(i, side, True)
-
-    def to_relay(i, side):
-        near, away = ((3, 0), (ncol - 4, ncol - 1))[side]
-        return pltpu.make_async_remote_copy(
-            src_ref=sb.at[chunk_of(i)], dst_ref=held.at[i // 2],
-            send_sem=one_send.at[side], recv_sem=held_recv.at[i // 2],
-            device_id=(row, jnp.where(lax.rem(i, 2) == 0, near, away)), device_id_type=MESH,
-        )
-
-    def from_relay(j, side, i):
-        return pltpu.make_async_remote_copy(
-            src_ref=held.at[j], dst_ref=(l2, r2)[side].at[chunk_of(i)],
-            send_sem=held_send, recv_sem=one_recv.at[side, i],
-            device_id=(row, relay_to), device_id_type=MESH,
-        )
-
-    def second_message(i, side):
-        lat = chunk_of(i)
-        lanes = (pl.ds(128, 128), pl.ds(0, 128))[side]
-        return pltpu.make_async_remote_copy(
-            src_ref=(l2, r2)[side].at[lat, :, lanes],
-            dst_ref=far.at[lat, :, pl.ds(side * 128, 128)],
-            send_sem=two_send.at[side], recv_sem=rest_recv.at[side, i],
-            device_id=(right, left)[side], device_id_type=MESH,
-        )
-
-    def send_near(start, stop):
-        def one(i, carry):
-            @pl.when(next_right)
-            def _():
-                first_message(i, 0).start()
-
-            @pl.when(next_left)
-            def _():
-                first_message(i, 1).start()
-
-            return carry
-
-        lax.fori_loop(start, stop, one, 0)
-
-    def send_far(start, stop, by):
-        def one(n, carry):
-            i = start + n * by
-
-            @pl.when(col == edge)
-            def _():
-                to_relay(i, 0).start()
-
-            @pl.when(col == edge + 1)
-            def _():
-                to_relay(i, 1).start()
-
-            return carry
-
-        lax.fori_loop(0, (stop - start + by - 1) // by, one, 0)
-
-    def send_rest(start, stop):
-        def one(i, carry):
-            @pl.when(next_right)
-            def _():
-                piece(i, 0, False).start()
-
-            @pl.when(next_left)
-            def _():
-                piece(i, 1, False).start()
-
-            return carry
-
-        lax.fori_loop(start, stop, one, 0)
-
-    @pl.when(jnp.logical_not(has_up))
-    def _():
-        buf0[pl.ds(0, STEPS)] = jnp.zeros((STEPS, nlon, width), F32)
-
-    @pl.when(jnp.logical_not(has_down))
-    def _():
-        buf0[pl.ds(strip + STEPS, STEPS)] = jnp.zeros((STEPS, nlon, width), F32)
-
-    @pl.when(jnp.logical_not(has_left))
-    def _():
-        l2[...] = jnp.zeros(l2.shape, BF16)
-
-    @pl.when(jnp.logical_not(has_right))
-    def _():
-        r2[...] = jnp.zeros(r2.shape, BF16)
-
-    @pl.when(col <= 1)
-    def _():
-        far[:, :, 0:128] = jnp.zeros((strip, nlon, 128), BF16)
-
-    @pl.when(col >= ncol - 2)
-    def _():
-        far[:, :, 128:256] = jnp.zeros((strip, nlon, 128), BF16)
+    def greeted():
+        pl.semaphore_wait(barrier, count)
+
+    @pl.when(far_relay)
+    def _():
+        greeted()
+        pl.semaphore_signal(ready, inc=1, device_id=(row, relay_from), device_id_type=MESH)
 
     for copy in small:
         copy.wait()
@@ -262,6 +143,132 @@
     rows_step(buf0, buf1, 0, 4, 10, 0)
     rows_step(buf1, buf2, 1, 5, 9, 0)
     rows_step(buf2, low, 2, 6, 8, STEPS)
+    @pl.when(jnp.logical_not(far_relay))
+    def _():
+        greeted()
+
+    to_near = pltpu.make_async_remote_copy(
+        src_ref=cov.at[pl.ds(jnp.where(even, strip - STEPS, 0), STEPS)],
+        dst_ref=buf0.at[pl.ds(jnp.where(even, 0, strip + STEPS), STEPS)],
+        send_sem=row_send.at[0], recv_sem=row_recv.at[0], device_id=near_row, device_id_type=MESH,
+    )
+    to_next = pltpu.make_async_remote_copy(
+        src_ref=edge_out, dst_ref=edge_in,
+        send_sem=row_send.at[1], recv_sem=row_recv.at[1], device_id=next_row, device_id_type=MESH,
+    )
+
+    @pl.when(has_next)
+    def _():
+        to_next.start()
+
+    to_near.start()
+
+    def piece(i, side, near):
+        lat = chunk_of(i)
+        lanes = pl.ds(128 if (side == 0) == near else 0, 128)
+        recv = one_recv if near else rest_recv
+        return pltpu.make_async_remote_copy(
+            src_ref=sb.at[lat, :, lanes], dst_ref=(l2, r2)[side].at[lat, :, lanes],
+            send_sem=one_send.at[side], recv_sem=recv.at[side, i],
+            device_id=(right, left)[side], device_id_type=MESH,
+        )
+
+    def first_message(i, side):
+        return piece(i, side, True)
+
+    def to_relay(i, side):
+        near, away = ((3, 0), (ncol - 4, ncol - 1))[side]
+        return pltpu.make_async_remote_copy(
+            src_ref=sb.at[chunk_of(i)], dst_ref=held.at[i // 2],
+            send_sem=one_send.at[side], recv_sem=held_recv.at[i // 2],
+            device_id=(row, jnp.where(lax.rem(i, 2) == 0, near, away)), device_id_type=MESH,
+        )
+
+    def from_relay(j, side, i):
+        return pltpu.make_async_remote_copy(
+            src_ref=held.at[j], dst_ref=(l2, r2)[side].at[chunk_of(i)],
+            send_sem=held_send, recv_sem=one_recv.at[side, i],
+            device_id=(row, relay_to), device_id_type=MESH,
+        )
+
+    def second_message(i, side):
+        lat = chunk_of(i)
+        lanes = (pl.ds(128, 128), pl.ds(0, 128))[side]
+        return pltpu.make_async_remote_copy(
+            src_ref=(l2, r2)[side].at[lat, :, lanes],
+            dst_ref=far.at[lat, :, pl.ds(side * 128, 128)],
+            send_sem=two_send.at[side], recv_sem=two_recv.at[side, i],
+            device_id=(right, left)[side], device_id_type=MESH,
+        )
+
+    def send_near(start, stop):
+        def one(i, carry):
+            @pl.when(next_right)
+            def _():
+                first_message(i, 0).start()
+
+            @pl.when(next_left)
+            def _():
+                first_message(i, 1).start()
+
+            return carry
+
+        lax.fori_loop(start, stop, one, 0)
+
+    def send_far(start, stop, by):
+        def one(n, carry):
+            i = start + n * by
+
+            @pl.when(col == edge)
+            def _():
+                to_relay(i, 0).start()
+
+            @pl.when(col == edge + 1)
+            def _():
+                to_relay(i, 1).start()
+
+            return carry
+
+        lax.fori_loop(0, (stop - start + by - 1) // by, one, 0)
+
+    def send_rest(start, stop):
+        def one(i, carry):
+            @pl.when(next_right)
+            def _():
+                piece(i, 0, False).start()
+
+            @pl.when(next_left)
+            def _():
+                piece(i, 1, False).start()
+
+            return carry
+
+        lax.fori_loop(start, stop, one, 0)
+
+    @pl.when(jnp.logical_not(has_up))
+    def _():
+        buf0[pl.ds(0, STEPS)] = jnp.zeros((STEPS, nlon, width), F32)
+
+    @pl.when(jnp.logical_not(has_down))
+    def _():
+        buf0[pl.ds(strip + STEPS, STEPS)] = jnp.zeros((STEPS, nlon, width), F32)
+
+    @pl.when(jnp.logical_not(has_left))
+    def _():
+        l2[...] = jnp.zeros(l2.shape, BF16)
+
+    @pl.when(jnp.logical_not(has_right))
+    def _():
+        r2[...] = jnp.zeros(r2.shape, BF16)
+
+    @pl.when(col <= 1)
+    def _():
+        far[:, :, 0:128] = jnp.zeros((strip, nlon, 128), BF16)
+
+    @pl.when(col >= ncol - 2)
+    def _():
+        far[:, :, 128:256] = jnp.zeros((strip, nlon, 128), BF16)
+
     send_near(0, 2)
     send_far(0, 1, 1)
     send_rest(0, 2)
@@ -286,7 +293,7 @@
     def pass_from_relay(i, side):
         return pltpu.make_async_remote_copy(
             src_ref=held_far.at[i], dst_ref=far.at[chunk_of(i), :, pl.ds(side * 128, 128)],
-            send_sem=far_send, recv_sem=rest_recv.at[side, i],
+            send_sem=far_send, recv_sem=two_recv.at[side, i],
             device_id=(row, relay_to), device_id_type=MESH,
         )
 
@@ -303,40 +310,28 @@
             def _():
                 pass_to_relay(i, side).start()
 
-    def arrival(like, recv):
-        return pltpu.make_async_remote_copy(
-            src_ref=like, dst_ref=like, send_sem=held_send, recv_sem=recv,
-            device_id=right, device_id_type=MESH,
-        )
-
     def departure(like, send):
         return pltpu.make_async_remote_copy(
             src_ref=like, dst_ref=like, send_sem=send, recv_sem=far_recv.at[0],
             device_id=right, device_id_type=MESH,
         )
 
+    def dot(x, w):
+        return jnp.dot(x, w, preferred_element_type=F32)
+
     def columns(i):
         lat = chunk_of(i)
 
-        for side, rest, passed in ((0, next_left, col > 1), (1, next_right, col < ncol - 2)):
-
-            @pl.when(rest & passed)
-            def _(side=side):
-                arrival(sb.at[lat], rest_recv.at[side, i]).wait_recv()
-
-            @pl.when(rest & jnp.logical_not(passed))
-            def _(side=side):
-                piece(i, side, False).wait_recv()
-
-            @pl.when(passed & jnp.logical_not(rest))
-            def _(side=side):
-                second_message(i, side).wait_recv()
-
-        def dot(x, w):
-            return jnp.dot(x, w, preferred_element_type=F32)
+        @pl.when(next_left)
+        def _():
+            piece(i, 0, False).wait_recv()
+
+        @pl.when(next_right)
+        def _():
+            piece(i, 1, False).wait_recv()
 
         total = dot(low[lat], w_high[2])
-        for place, ref in enumerate((far, l2, sb, r2)):
+        for place, ref in ((1, l2), (2, sb), (3, r2)):
             x = ref[lat]
             total = total + dot(x, w_high[place]) + dot(x, w_low[place])
         ob[lat] = total
@@ -350,6 +345,20 @@
                 )
                 line = noise[pl.ds(lat, 1), :]
                 ob[lat, :, lanes] = ob[lat, :, lanes] + jnp.where(own, line, 0.0)
+
+    def far_columns(i):
+        lat = chunk_of(i)
+
+        @pl.when(col > 1)
+        def _():
+            second_message(i, 0).wait_recv()
+
+        @pl.when(col < ncol - 2)
+        def _():
+            second_message(i, 1).wait_recv()
+
+        x = far[lat]
+        ob[lat] = ob[lat] + dot(x, w_high[0]) + dot(x, w_low[0])
 
     def relay_turn(i):
         for side, here in ((0, lower), (1, jnp.logical_not(lower))):
@@ -457,13 +466,16 @@
         return carry
 
     def last_turn(i, carry):
+        stop = jnp.where(i < JOINT, i + 1, jnp.where(i == JOINT, strip, i))
+        lax.fori_loop(i, stop, edge_turn, 0)
+
         @pl.when(i < strip)
         def _():
-            edge_turn(i, 0)
+            columns(i)
 
         @pl.when(i >= LAG)
         def _():
-            columns(i - LAG)
+            far_columns(i - LAG)
 
         return carry
 
@@ -495,10 +507,10 @@
 
 
 def write_out(out_in, s_in, out, s, sem):
-    copies = []
-    for lat in range(out.shape[0]):
-        copies.append(pltpu.make_async_copy(out_in.at[lat], out.at[lat], sem.at[0, lat]))
-        copies.append(pltpu.make_async_copy(s_in.at[lat], s.at[lat], sem.at[1, lat]))
+    copies = [
+        pltpu.make_async_copy(out_in, out, sem.at[0, 0]),
+        pltpu.make_async_copy(s_in, s, sem.at[1, 0]),
+    ]
     for copy in copies:
         copy.start()
     for copy in copies:
@@ -548,6 +560,7 @@
                 pltpu.SemaphoreType.DMA((2, strip)),
                 pltpu.SemaphoreType.DMA((2, strip)),
                 pltpu.SemaphoreType.DMA((2,)),
+                pltpu.SemaphoreType.DMA((2, strip)),
                 pltpu.SemaphoreType.DMA,
                 pltpu.SemaphoreType.DMA((strip // 2,)),
                 pltpu.SemaphoreType.DMA,
@@ -563,7 +576,7 @@
             out_shape=(jax.ShapeDtypeStruct(block, F32), jax.ShapeDtypeStruct(block, BF16)),
             in_specs=[pl.BlockSpec(memory_space=pltpu.VMEM)] * 2,
             out_specs=(anywhere, anywhere),
-            scratch_shapes=[pltpu.SemaphoreType.DMA((2, strip))],
+            scratch_shapes=[pltpu.SemaphoreType.DMA((2, 1))],
             compiler_params=pltpu.CompilerParams(vmem_limit_bytes=1 << 20),
         )(held_out, held_s)
         return out.reshape(rows_dev, cols_dev), s.reshape(rows_dev, cols_dev)

time: 33.3 us -> 33.2 us (level)
  no operation moved by 1% of the time
where the time goes in v7:
time: 33.2 us; the launch traced here: 33.1 us
  Pallas kernels  32.4 us (98%)
  between operations  0.64 us (2%)
    pallas_call x1, Pallas kernels, body(): pl.pallas_call(functools.partial(kernel, nlat, nrow, ncol), out_shape=(ja...  31.3 us
    pallas_call x1, Pallas kernels, body(): pl.pallas_call(write_out, out_shape=(jax.ShapeDtypeStruct(block, F32), ja...  1.16 us

profile of v7, /device:TPU:54, one launch (start us, length us, event | category | flops | bytes accessed | tf_op | source)
XLA Modules:
  0.0 33.1 jit_solution(14416661135127907847)
XLA Ops:
  0.6 31.3 %shard_map.68 = (f32[8,128,256]{2,1,0:T(8,128)S(1)}, bf16[8,128,256]{2,1,0:T(8,128)(2,1)S(1)}) custom-call(f32[8,128,256]{2,1,0:T(8,128)} %bitcast.4, f32[8,128]{1,0:T(8,128)} %noise_in.1, f32[2,16]{1,0:T(2,128)} %bitcast.5, f32[16]{0:T(128)} %diffusivity_in.1, s32[3,64]{1,0:T(4,128)} %index_in.1), custom_call_target="tpu_custom_call" | custom-call | tf_op jit(solution)/shard_map/pallas_call | solution.py:530
  31.9 1.2 %shard_map.69 = (f32[8,128,256]{2,1,0:T(8,128)}, bf16[8,128,256]{2,1,0:T(8,128)(2,1)}) custom-call(f32[8,128,256]{2,1,0:T(8,128)S(1)} %get-tuple-element.6.out_in, bf16[8,128,256]{2,1,0:T(8,128)(2,1)S(1)} %get-tuple-element.7.s_in), custom_call_target="tpu_custom_call" | custom-call | tf_op jit(solution)/shard_map/pallas_call | solution.py:574

commit v8 on v7

--- a/solution.py
+++ b/solution.py
@@ -101,6 +101,14 @@
             pl.semaphore_signal(barrier, inc=1, device_id=peer, device_id_type=MESH)
 
         count = count + jnp.where(there, 1, 0)
+
+    def greeted():
+        pl.semaphore_wait(barrier, count)
+
+    @pl.when(far_relay)
+    def _():
+        greeted()
+        pl.semaphore_signal(ready, inc=1, device_id=(row, relay_from), device_id_type=MESH)
 
     load.wait()
     edge_out[...] = buf0[pl.ds(jnp.where(even, STEPS, strip), STEPS)].astype(BF16)
@@ -128,14 +136,6 @@
             return carry
 
         lax.fori_loop(first, last, one, 0)
-
-    def greeted():
-        pl.semaphore_wait(barrier, count)
-
-    @pl.when(far_relay)
-    def _():
-        greeted()
-        pl.semaphore_signal(ready, inc=1, device_id=(row, relay_from), device_id_type=MESH)
 
     for copy in small:
         copy.wait()

time: 33.2 us -> 33.1 us (level)
  no operation moved by 1% of the time
where the time goes in v8:
time: 33.1 us; the launch traced here: 33 us
  Pallas kernels  32.4 us (98%)
  between operations  0.64 us (2%)
    pallas_call x1, Pallas kernels, body(): pl.pallas_call(functools.partial(kernel, nlat, nrow, ncol), out_shape=(ja...  31.2 us
    pallas_call x1, Pallas kernels, body(): pl.pallas_call(write_out, out_shape=(jax.ShapeDtypeStruct(block, F32), ja...  1.16 us

profile of v8, /device:TPU:54, one launch (start us, length us, event | category | flops | bytes accessed | tf_op | source)
XLA Modules:
  0.0 33.0 jit_solution(14519265952997542404)
XLA Ops:
  0.6 31.2 %shard_map.68 = (f32[8,128,256]{2,1,0:T(8,128)S(1)}, bf16[8,128,256]{2,1,0:T(8,128)(2,1)S(1)}) custom-call(f32[8,128,256]{2,1,0:T(8,128)} %bitcast.4, f32[8,128]{1,0:T(8,128)} %noise_in.1, f32[2,16]{1,0:T(2,128)} %bitcast.5, f32[16]{0:T(128)} %diffusivity_in.1, s32[3,64]{1,0:T(4,128)} %index_in.1), custom_call_target="tpu_custom_call" | custom-call | tf_op jit(solution)/shard_map/pallas_call | solution.py:530
  31.9 1.2 %shard_map.69 = (f32[8,128,256]{2,1,0:T(8,128)}, bf16[8,128,256]{2,1,0:T(8,128)(2,1)}) custom-call(f32[8,128,256]{2,1,0:T(8,128)S(1)} %get-tuple-element.6.out_in, bf16[8,128,256]{2,1,0:T(8,128)(2,1)S(1)} %get-tuple-element.7.s_in), custom_call_target="tpu_custom_call" | custom-call | tf_op jit(solution)/shard_map/pallas_call | solution.py:574

commit v9 on v8

--- a/solution.py
+++ b/solution.py
@@ -12,7 +12,7 @@
 BF16 = jnp.bfloat16
 STEPS = 3
 LAG = 3
-JOINT = 5
+JOINT = 3
 
 
 def chunk_of(i):
@@ -43,7 +43,7 @@
     cov, noise_in, table_in, diffusivity_in, index_in,
     ob, sb,
     buf0, buf1, buf2, low, l2, r2, far, held, held_far, edge_out, edge_in, w_high, w_low, noise, table, diffusivity, index, weights,
-    ready, load_sem, small_sem, row_send, row_recv, one_send, one_recv, rest_recv, two_send, two_recv, held_send, held_recv, far_send, far_recv,
+    ready, load_sem, small_sem, row_send, row_recv, one_send, one_recv, rest_recv, two_send, two_recv, held_send, far_send, far_recv,
 ):
     strip, nlon, width = cov.shape
     row, col = lax.axis_index("row"), lax.axis_index("col")
@@ -180,7 +180,7 @@
         near, away = ((3, 0), (ncol - 4, ncol - 1))[side]
         return pltpu.make_async_remote_copy(
             src_ref=sb.at[chunk_of(i)], dst_ref=held.at[i // 2],
-            send_sem=one_send.at[side], recv_sem=held_recv.at[i // 2],
+            send_sem=one_send.at[side], recv_sem=far_recv.at[i // 2],
             device_id=(row, jnp.where(lax.rem(i, 2) == 0, near, away)), device_id_type=MESH,
         )
 
@@ -562,7 +562,6 @@
                 pltpu.SemaphoreType.DMA((2,)),
                 pltpu.SemaphoreType.DMA((2, strip)),
                 pltpu.SemaphoreType.DMA,
-                pltpu.SemaphoreType.DMA((strip // 2,)),
                 pltpu.SemaphoreType.DMA,
                 pltpu.SemaphoreType.DMA((strip,)),
             ],

time: 33.1 us -> 33.2 us (level)
  no operation moved by 1% of the time
where the time goes in v9:
time: 33.2 us; the launch traced here: 33 us
  Pallas kernels  32.4 us (98%)
  between operations  0.64 us (2%)
    pallas_call x1, Pallas kernels, body(): pl.pallas_call(functools.partial(kernel, nlat, nrow, ncol), out_shape=(ja...  31.2 us
    pallas_call x1, Pallas kernels, body(): pl.pallas_call(write_out, out_shape=(jax.ShapeDtypeStruct(block, F32), ja...  1.16 us

profile of v9, /device:TPU:54, one launch (start us, length us, event | category | flops | bytes accessed | tf_op | source)
XLA Modules:
  0.0 33.0 jit_solution(9161296848125762976)
XLA Ops:
  0.6 31.2 %shard_map.68 = (f32[8,128,256]{2,1,0:T(8,128)S(1)}, bf16[8,128,256]{2,1,0:T(8,128)(2,1)S(1)}) custom-call(f32[8,128,256]{2,1,0:T(8,128)} %bitcast.4, f32[8,128]{1,0:T(8,128)} %noise_in.1, f32[2,16]{1,0:T(2,128)} %bitcast.5, f32[16]{0:T(128)} %diffusivity_in.1, s32[3,64]{1,0:T(4,128)} %index_in.1), custom_call_target="tpu_custom_call" | custom-call | tf_op jit(solution)/shard_map/pallas_call | solution.py:530
  31.8 1.2 %shard_map.69 = (f32[8,128,256]{2,1,0:T(8,128)}, bf16[8,128,256]{2,1,0:T(8,128)(2,1)}) custom-call(f32[8,128,256]{2,1,0:T(8,128)S(1)} %get-tuple-element.6.out_in, bf16[8,128,256]{2,1,0:T(8,128)(2,1)S(1)} %get-tuple-element.7.s_in), custom_call_target="tpu_custom_call" | custom-call | tf_op jit(solution)/shard_map/pallas_call | solution.py:573
